TPU v7x, 512 devices: a whole 4x4x16 slice. The times are simulated.
512 devices in a mesh: bead: 32 (over x, z_lo), space: 16 (over y, z_hi, core).
Axes of the slice: x: 4, y: 4, z: 16 (z_hi: 2, z_lo: 8; z = z_hi * 8 + z_lo), core: 2. Of those that a mesh axis runs over, the one named last changes fastest.
Arguments:
- positions: float32 [32, 256, 3, 128], P('bead', 'space'), may hold values from 0 to 1
- momenta: float32 [32, 256, 3, 128], P('bead', 'space'), may hold values from -3 to 3
- noise: float32 [32, 256, 3, 128], P('bead', 'space'), may hold values from -6 to 6
- atom_types: int32 [256, 128], P('space'), may hold values from 0 to 3
- occupancy: int32 [256], P('space'), may hold values from 64 to 128, as said below
- type_sigma: float32 [4], replicated, may hold values from 0.2 to 0.4
- type_eps: float32 [4], replicated, may hold values from 0.5 to 2
- type_mass: float32 [4], replicated, may hold values from 1 to 4
Outputs:
- new_positions: float32 [32, 256, 3, 128], P('bead', 'space')
- new_momenta: float32 [32, 256, 3, 128], P('bead', 'space')
Inputs may be any that keep to these rules, and one draw needn't show every extreme that they name: `occupancy`: in each domain of 16 consecutive cells some cell holds 128 atoms.
All inputs are finite; a program needn't handle non-finite values.
Results may differ from a plain program's by a relative error of at most 0.0002.
Values sent between devices are 32-bit elements; how exact they have to be, the bound alone decides.
A program may use at most 64 MiB of HBM per device.

v0:
```python
import jax
import jax.numpy as jnp
from jax import lax
from jax.sharding import PartitionSpec as P

PC = 8
GY = 4
GZ = 4


TIME_STEP = 0.05
INVERSE_TEMP = 32.0
CENTROID_FRICTION = 1.0
INNER_CUT = 0.5
OUTER_CUT = 1.0
precise = lax.Precision.HIGHEST


def with_halo(cells, sides, width):
    for axis, dim in sides:
        count = lax.axis_size(axis)
        head = lax.slice_in_dim(cells, 0, width, axis=dim)
        tail = lax.slice_in_dim(cells, cells.shape[dim] - width, cells.shape[dim], axis=dim)
        cells = jnp.concatenate(
            [
                lax.ppermute(tail, axis, [(i, (i + 1) % count) for i in range(count)]),
                cells,
                lax.ppermute(head, axis, [((i + 1) % count, i) for i in range(count)]),
            ],
            axis=dim,
        )
    return cells


def joined_along(blocks, dim):
    blocks = jnp.moveaxis(blocks, 0, dim)
    shape = blocks.shape
    return blocks.reshape(*shape[:dim], shape[dim] * shape[dim + 1], *shape[dim + 2 :])


def sent_to_all(value, axis):
    copies = jnp.broadcast_to(value, (lax.axis_size(axis), *value.shape))
    return lax.all_to_all(copies, axis, split_axis=0, concat_axis=0, tiled=True)


def collect_2(value, axis, dim):
    return joined_along(sent_to_all(value, axis), dim)


def stencil_table(cell_total, per_domain, depth_z, height_y):
    in_domain = jnp.arange(cell_total) % per_domain
    across = in_domain // depth_z
    upward = in_domain % depth_z
    offsets = jnp.arange(27)
    step_x = offsets // 9 - 1
    step_y = offsets // 3 % 3 - 1
    step_z = offsets % 3 - 1
    target_y = across[:, None] + step_y[None, :]
    target_z = upward[:, None] + step_z[None, :]
    inside = (target_y >= 0) & (target_y < height_y) & (target_z >= 0) & (target_z < depth_z)
    entry = (step_x[None, :] + 1) * per_domain + target_y * depth_z + target_z
    return jnp.where(inside, entry, 3 * per_domain)


def mode_table(number):
    bead_rows = jnp.arange(number, dtype=jnp.float32)[:, None]
    column = jnp.arange(number, dtype=jnp.float32)[None, :]
    phases = 2.0 * jnp.pi * bead_rows * column / number
    factor = jnp.sqrt(2.0 / number)
    middle = jnp.cos(jnp.pi * bead_rows) / jnp.sqrt(float(number))
    matrix = jnp.where(column < number / 2, factor * jnp.cos(phases), factor * jnp.sin(phases))
    matrix = jnp.where(column == number / 2, middle, matrix)
    matrix = jnp.where(column == 0, 1.0 / jnp.sqrt(float(number)), matrix)
    return matrix


def contract_table(full_count, reduced):
    selected = jnp.arange(reduced)
    selected = jnp.where(selected <= reduced // 2, selected, selected + full_count - reduced)
    chosen = mode_table(full_count)[:, selected]
    product = jnp.dot(
        mode_table(reduced), chosen.T, precision=precise, preferred_element_type=jnp.float32
    )
    return jnp.sqrt(reduced / full_count) * product


def propagate(position_modes, momentum_modes, noise_modes):
    number = position_modes.shape[0]
    mode_index = jnp.arange(number)
    frequency = (
        2.0 * (number / INVERSE_TEMP) * jnp.sin(jnp.pi * mode_index.astype(jnp.float32) / number)
    )
    friction = jnp.where(mode_index == 0, CENTROID_FRICTION, 2.0 * frequency)
    damping = jnp.exp(-friction * TIME_STEP)
    kicking = jnp.sqrt((1.0 - damping * damping) / INVERSE_TEMP)
    cosine = jnp.cos(frequency * TIME_STEP)
    sine_term = jnp.sin(frequency * TIME_STEP)
    drift_factor = jnp.where(
        mode_index == 0, TIME_STEP, sine_term / jnp.where(mode_index == 0, 1.0, frequency)
    )
    spring = frequency * sine_term
    trailing = (number,) + (1,) * (position_modes.ndim - 1)
    damping = damping.reshape(trailing)
    kicking = kicking.reshape(trailing)
    cosine = cosine.reshape(trailing)
    drift_factor = drift_factor.reshape(trailing)
    spring = spring.reshape(trailing)
    momentum = damping * momentum_modes + kicking * noise_modes
    next_position = cosine * position_modes + drift_factor * momentum
    next_momentum = cosine * momentum - spring * position_modes
    return (next_position, next_momentum)


def atom_table(atom_types, occupancy, type_sigma, type_eps, type_mass):
    type_codes = jnp.arange(type_sigma.shape[0])
    onehot = (atom_types[..., None] == type_codes).astype(jnp.float32)
    sigma_atom = jnp.sum(onehot * type_sigma, -1)
    energy_root = jnp.sqrt(jnp.sum(onehot * type_eps, -1))
    mass_atom = jnp.sum(onehot * type_mass, -1)
    slot_index = jnp.arange(atom_types.shape[-1])
    living = (slot_index[None, :] < occupancy[:, None]).astype(jnp.float32)
    return (jnp.stack([sigma_atom, energy_root, living], 1), mass_atom)


def anchor_of(ext_index, domain_cells, slab_depth):
    slab_layer = ext_index // domain_cells - 1
    within = ext_index % domain_cells
    return jnp.stack([slab_layer, within // slab_depth, within % slab_depth], -1).astype(
        jnp.float32
    )


def taper(radius_sq, cutoff):
    margin = jnp.maximum(0.0, 1.0 - radius_sq / (cutoff * cutoff))
    return (margin * margin, -2.0 * margin / (cutoff * cutoff))


def pair_force(left_position, left_param, right_position, right_param, longer):
    separation = left_position[:, :, None] - right_position[:, None, :]
    radius_sq = jnp.sum(separation * separation, 0)
    sigma_pair = 0.5 * (left_param[0][:, None] + right_param[0][None, :])
    sigma_sq = sigma_pair * sigma_pair
    energy = left_param[1][:, None] * right_param[1][None, :]
    shifted = radius_sq + sigma_sq
    quotient = sigma_sq / shifted
    sixth_power = quotient * quotient * quotient
    potential = 4.0 * energy * (sixth_power * sixth_power - sixth_power)
    derivative = -12.0 * energy * (2.0 * sixth_power - 1.0) * sixth_power / shifted
    outer_value, outer_slope = taper(radius_sq, OUTER_CUT)
    inner_value, inner_slope = taper(radius_sq, INNER_CUT)
    if longer:
        switch = outer_value - inner_value
        switch_slope = outer_slope - inner_slope
    else:
        switch = inner_value
        switch_slope = inner_slope
    weight = -2.0 * (derivative * switch + potential * switch_slope)
    weight = weight * left_param[2][:, None] * right_param[2][None, :]
    return jnp.sum(weight[None] * separation, 2)


def row_force(absolute, ext_params, listing_table, bead_pick, cell_pick, longer):
    domain_cells = listing_table.shape[0]
    listing = listing_table[cell_pick]
    left_position = absolute[bead_pick, cell_pick + domain_cells]
    left_param = ext_params[cell_pick + domain_cells]
    right_position = jnp.transpose(absolute[bead_pick][listing], (1, 0, 2)).reshape(3, -1)
    right_param = jnp.transpose(ext_params[listing], (1, 0, 2)).reshape(3, -1)
    return pair_force(left_position, left_param, right_position, right_param, longer)


def shards(positions, momenta, noise, atom_types, occupancy, type_sigma, type_eps, type_mass):
    local_beads = positions.shape[0]
    domain_cells = positions.shape[1]
    slot_count = positions.shape[3]
    bead_count = lax.axis_size("bead")
    bead_rank = lax.axis_index("bead")
    total_beads = local_beads * bead_count
    listing_table = stencil_table(domain_cells, domain_cells, GZ, GY)
    params, mass_atom = atom_table(atom_types, occupancy, type_sigma, type_eps, type_mass)
    root_mass = jnp.sqrt(mass_atom)[None, :, None, :]
    ext_anchor = anchor_of(jnp.arange(3 * domain_cells + 1), domain_cells, GZ)[None, :, :, None]
    stacked = jnp.concatenate([positions, params[None]], 0)
    widened = with_halo(stacked, (("space", 1),), domain_cells)
    widened = jnp.concatenate([widened, jnp.zeros_like(widened[:, :1])], 1)
    absolute = widened[:-1] + ext_anchor
    ext_params = widened[-1]

    def short_row(row_index):
        return row_force(
            absolute,
            ext_params,
            listing_table,
            row_index // domain_cells,
            row_index % domain_cells,
            False,
        )

    short_force = lax.map(short_row, jnp.arange(local_beads * domain_cells)).reshape(
        positions.shape
    )
    kicked = momenta + 0.5 * TIME_STEP * short_force
    scaled_position = positions * root_mass
    scaled_momentum = kicked / root_mass
    matrix = mode_table(total_beads)
    pieces = domain_cells * 3 * slot_count // bead_count
    shaped = (
        scaled_position.reshape(local_beads, bead_count, pieces),
        scaled_momentum.reshape(local_beads, bead_count, pieces),
        noise.reshape(local_beads, bead_count, pieces),
    )
    position_modes = jnp.einsum(
        "kn,kij->nij",
        matrix,
        lax.all_to_all(shaped[0], "bead", split_axis=1, concat_axis=0, tiled=True),
        precision=precise,
    )
    momentum_modes = jnp.einsum(
        "kn,kij->nij",
        matrix,
        lax.all_to_all(shaped[1], "bead", split_axis=1, concat_axis=0, tiled=True),
        precision=precise,
    )
    noise_modes = jnp.einsum(
        "kn,kij->nij",
        matrix,
        lax.all_to_all(shaped[2], "bead", split_axis=1, concat_axis=0, tiled=True),
        precision=precise,
    )
    moved_position, moved_momentum = propagate(position_modes, momentum_modes, noise_modes)
    back_position = jnp.einsum("kn,nij->kij", matrix, moved_position, precision=precise)
    back_momentum = jnp.einsum("kn,nij->kij", matrix, moved_momentum, precision=precise)
    moved_x = lax.all_to_all(back_position, "bead", split_axis=0, concat_axis=1, tiled=True)
    moved_p = lax.all_to_all(back_momentum, "bead", split_axis=0, concat_axis=1, tiled=True)
    bead_position = moved_x.reshape(positions.shape)
    bead_momentum = moved_p.reshape(positions.shape)
    new_positions = bead_position / root_mass
    free_momenta = bead_momentum * root_mass
    weights = contract_table(total_beads, PC)
    reduced = weights.shape[0]
    held_groups = max(1, reduced // bead_count)
    row_total = reduced * domain_cells // bead_count
    cell_span = row_total // held_groups
    first_group = bead_rank * reduced // bead_count
    first_cell = bead_rank * row_total % domain_cells
    own_columns = lax.dynamic_slice_in_dim(weights, bead_rank * local_beads, local_beads, 1)
    chosen_rows = lax.dynamic_slice_in_dim(weights, first_group, held_groups, 0)
    chosen = jnp.einsum(
        "rk,kcda->rcda", chosen_rows, collect_2(new_positions, "bead", 0), precision=precise
    )
    stacked_slow = jnp.concatenate([chosen, params[None]], 0)
    widened_slow = with_halo(stacked_slow, (("space", 1),), domain_cells)
    widened_slow = jnp.concatenate([widened_slow, jnp.zeros_like(widened_slow[:, :1])], 1)
    absolute_slow = widened_slow[:-1] + ext_anchor
    params_slow = widened_slow[-1]

    def slow_row(row_index):
        return row_force(
            absolute_slow,
            params_slow,
            listing_table,
            row_index // cell_span,
            first_cell + row_index % cell_span,
            True,
        )

    slow_rows = lax.map(slow_row, jnp.arange(row_total))
    own_weights = own_columns.T
    arrived = collect_2(slow_rows, "bead", 0)
    number = arrived.shape[0]
    global_rows = jnp.arange(number)
    group_hot = (global_rows[None, :] // domain_cells == jnp.arange(reduced)[:, None]).astype(
        jnp.float32
    )
    cell_hot = (global_rows[None, :] % domain_cells == jnp.arange(domain_cells)[:, None]).astype(
        jnp.float32
    )
    coeffs = jnp.dot(own_weights, group_hot, precision=precise, preferred_element_type=jnp.float32)
    mixing = (coeffs[:, None, :] * cell_hot[None]).reshape(local_beads * domain_cells, number)
    slow_total = jnp.dot(
        mixing, arrived.reshape(number, -1), precision=precise, preferred_element_type=jnp.float32
    )
    spread_force = total_beads / reduced * slow_total.reshape(positions.shape)
    new_momenta = free_momenta + 0.5 * TIME_STEP * spread_force
    return (new_positions, new_momenta)


def solution(mesh):
    placed = (
        P("bead", "space", None, None),
        P("bead", "space", None, None),
        P("bead", "space", None, None),
        P("space", None),
        P("space"),
        P(),
        P(),
        P(),
    )
    return jax.shard_map(
        shards,
        mesh=mesh,
        in_specs=placed,
        out_specs=(P("bead", "space", None, None), P("bead", "space", None, None)),
        check_vma=False,
    )
```

profile of v0, /device:TPU:6, one launch (start us, length us, event | category | flops | bytes accessed | tf_op | source)
XLA Modules:
  0.0 334.0 jit_solution(6240963295736827216)
XLA Ops:
  1.4 0.8 select_reduce_fusion.2
  2.2 0.7 pad_maximum_fusion.3
  2.9 17.6 %collective-permute-start.1 = (f32[2,16,3,128]{3,1,2,0:T(8,128)S(1)}, f32[2,16,3,128]{3,1,2,0:T(8,128)S(1)}, u32[]{:S(2)}, u32[]{:S(2)}) collective-permute-start(f32[2,16,3,128]{3,1,2,0:T(8,128)S(1)} %pad_maximum_fusion.3), channel_id=1, source_target_pairs={{1,0},{2,1},{3,2},{4,3},{5,4},{6,5},{7,6},{8,7},{9,8},{10,9},{11,1... | collective-permute-start | bytes 147464 | tf_op jit(solution)/shard_map/ppermute | solution.py:28
  20.5 1.9 collective-permute-start
  22.9 0.8 copy.48
  24.5 12.3 %collective-permute-done = f32[2,16,3,128]{3,1,2,0:T(8,128)S(1)} collective-permute-done((f32[2,16,3,128]{3,1,2,0:T(8,128)S(1)}, f32[2,16,3,128]{3,1,2,0:T(8,128)S(1)}, u32[]{:S(2)}, u32[]{:S(2)}) %collective-permute-start) | collective-permute-done | bytes 49184 | tf_op jit(solution)/shard_map/ppermute | solution.py:26
  36.8 0.8 fusion.33
  37.8 116.5 %while.24 = (s32[]{:T(128)}, f32[16,3,128]{2,1,0:T(4,128)S(1)}, s32[16]{0:T(128)S(1)}, f32[49,3,128]{2,1,0:T(4,128)S(1)}, s32[16,27]{1,0:T(8,128)S(1)}, /*index=...) while((s32[]{:T(128)}, f32[16,3,128]{2,1,0:T(4,128)S(1)}, ...), condition=%wide.region_6.7_spmd, body=%wide.region_3.6_spmd.sunk | while | flops 19907428 | bytes 7475550 | solution.py:199
  42.5 1.8 fusion.126
  49.0 0.7 fusion.125
  49.8 1.8 fusion.126
  57.0 1.8 fusion.126
  64.3 1.8 fusion.126
  71.6 1.8 fusion.126
  78.9 1.8 fusion.126
  86.2 1.8 fusion.126
  93.5 1.8 fusion.126
  100.7 1.8 fusion.126
  107.3 0.7 fusion.125
  108.0 1.8 fusion.126
  115.3 1.8 fusion.126
  122.6 1.8 fusion.126
  129.9 1.8 fusion.126
  137.1 1.8 fusion.126
  144.4 1.8 fusion.126
  151.7 1.8 fusion.126
  155.1 8.2 %all-to-all-start.1 = ((f32[1,32,192]{2,0,1:T(1,128)}), f32[1,32,192]{2,0,1:T(1,128)S(1)}, u32[]{:S(2)}, u32[]{:S(2)}) async-start(f32[1,32,192]{2,0,1:T(1,128)} %reshape.1027), calls=%async_computation.1 | async-start | bytes 65536 | tf_op jit(solution)/shard_map/all_to_all | solution.py:221
  164.0 9.9 %all-to-all-done.1 = f32[1,32,192]{2,0,1:T(1,128)S(1)} async-done(((f32[1,32,192]{2,0,1:T(1,128)}), f32[1,32,192]{2,0,1:T(1,128)S(1)}, u32[]{:S(2)}, u32[]{:S(2)}) %all-to-all-start.1) | async-done | bytes 24608 | tf_op jit(solution)/shard_map/all_to_all | solution.py:221
  173.9 5.7 %all-to-all-start = ((f32[1,32,192]{2,0,1:T(1,128)}), f32[1,32,192]{2,0,1:T(1,128)S(1)}, u32[]{:S(2)}, u32[]{:S(2)}) async-start(f32[1,32,192]{2,0,1:T(1,128)} %reshape.1026), calls=%async_computation | async-start | bytes 65536 | tf_op jit(solution)/shard_map/all_to_all | solution.py:215
  179.9 10.5 %all-to-all-done = f32[1,32,192]{2,0,1:T(1,128)S(1)} async-done(((f32[1,32,192]{2,0,1:T(1,128)}), f32[1,32,192]{2,0,1:T(1,128)S(1)}, u32[]{:S(2)}, u32[]{:S(2)}) %all-to-all-start) | async-done | bytes 24608 | tf_op jit(solution)/shard_map/all_to_all | solution.py:215
  190.3 5.8 %all-to-all-start.2 = ((f32[1,32,192]{2,0,1:T(1,128)}), f32[1,32,192]{2,0,1:T(1,128)S(1)}, u32[]{:S(2)}, u32[]{:S(2)}) async-start(f32[1,32,192]{2,0,1:T(1,128)} %reshape.1028), calls=%async_computation.2 | async-start | bytes 65536 | tf_op jit(solution)/shard_map/all_to_all | solution.py:227
  196.4 10.4 %all-to-all-done.2 = f32[1,32,192]{2,0,1:T(1,128)S(1)} async-done(((f32[1,32,192]{2,0,1:T(1,128)}), f32[1,32,192]{2,0,1:T(1,128)S(1)}, u32[]{:S(2)}, u32[]{:S(2)}) %all-to-all-start.2) | async-done | bytes 24608 | tf_op jit(solution)/shard_map/all_to_all | solution.py:227
  207.3 15.9 %all_to_all.55 = f32[32,1,192]{2,1,0:T(1,128)S(1)} all-to-all(f32[32,1,192]{2,1,0:T(1,128)S(1)} %copy.50), channel_id=1, replica_groups=mesh['bead'=32,'space'=16] {'bead'}, dimensions={0} | all-to-all | bytes 49152 | tf_op jit(solution)/shard_map/all_to_all | solution.py:233
  223.4 0.9 broadcast_in_dim.213
  224.3 5.8 %all-to-all-start.5 = ((f32[32,1,16,3,128]{4,2,3,1,0:T(8,128)}), f32[32,1,16,3,128]{4,2,3,1,0:T(8,128)S(1)}, u32[]{:S(2)}, u32[]{:S(2)}) async-start(f32[32,1,16,3,128]{4,2,3,1,0:T(8,128)} %broadcast_in_dim.213), calls=%async_computation.5 | async-start | bytes 1572864 | tf_op jit(solution)/shard_map/all_to_all | solution.py:43
  231.2 22.9 %all-to-all-done.5 = f32[32,1,16,3,128]{4,2,3,1,0:T(8,128)S(1)} async-done(((f32[32,1,16,3,128]{4,2,3,1,0:T(8,128)}), f32[32,1,16,3,128]{4,2,3,1,0:T(8,128)S(1)}, u32[]{:S(2)}, u32[]{:S(2)}) %all-to-all-start.5) | async-done | bytes 786464 | tf_op jit(solution)/shard_map/all_to_all | solution.py:43
  254.9 9.6 %collective-permute-start.3 = (f32[2,16,3,128]{3,1,2,0:T(8,128)S(1)}, f32[2,16,3,128]{3,1,2,0:T(8,128)S(1)}, u32[]{:S(2)}, u32[]{:S(2)}) collective-permute-start(f32[2,16,3,128]{3,1,2,0:T(8,128)S(1)} %pad_maximum_fusion.2), channel_id=1, source_target_pairs={{1,0},{2,1},{3,2},{4,3},{5,4},{6,5},{7,6},{8,7},{9,8},{10,9},{11,1... | collective-permute-start | bytes 147464 | tf_op jit(solution)/shard_map/ppermute | solution.py:28
  264.4 1.9 collective-permute-start.2
  267.3 8.3 %all-to-all-start.4 = ((f32[32,1,192]{2,1,0:T(1,128)}), f32[32,1,192]{2,1,0:T(1,128)S(1)}, u32[]{:S(2)}, u32[]{:S(2)}) async-start(f32[32,1,192]{2,1,0:T(1,128)} %copy.51), calls=%async_computation.4 | async-start | bytes 65536 | tf_op jit(solution)/shard_map/all_to_all | solution.py:234
  275.6 5.5 %collective-permute-done.2 = f32[2,16,3,128]{3,1,2,0:T(8,128)S(1)} collective-permute-done((f32[2,16,3,128]{3,1,2,0:T(8,128)S(1)}, f32[2,16,3,128]{3,1,2,0:T(8,128)S(1)}, u32[]{:S(2)}, u32[]{:S(2)}) %collective-permute-start.2) | collective-permute-done | bytes 49184 | tf_op jit(solution)/shard_map/ppermute | solution.py:26
  281.3 30.5 %while.25 = (s32[]{:T(128)}, f32[4,3,128]{2,0,1:T(4,128)S(1)}, s32[4]{0:T(128)S(1)}, s32[]{:T(128)}, f32[49,3,128]{2,1,0:T(4,128)S(1)}, /*index=5*/s32[16,27]{1,...) while((s32[]{:T(128)}, f32[4,3,128]{2,0,1:T(4,128)S(1)}, ...), condition=%wide.region_10.11_spmd, body=%wide.region_7.10_spmd.sunk | while | flops 22561636 | bytes 7477626 | solution.py:267
  286.0 2.1 fusion.130
  293.7 2.1 fusion.130
  301.3 2.1 fusion.130
  308.9 2.1 fusion.130
  312.5 8.0 %all-to-all-start.6 = ((f32[32,4,3,128]{3,1,2,0:T(4,128)}), f32[32,4,3,128]{3,1,2,0:T(4,128)S(1)}, u32[]{:S(2)}, u32[]{:S(2)}) async-start(f32[32,4,3,128]{3,1,2,0:T(4,128)} %broadcast_in_dim.214), calls=%async_computation.6 | async-start | bytes 393216 | tf_op jit(solution)/shard_map/all_to_all | solution.py:43
  321.7 11.1 %all-to-all-done.6 = f32[32,4,3,128]{3,1,2,0:T(4,128)S(1)} async-done(((f32[32,4,3,128]{3,1,2,0:T(4,128)}), f32[32,4,3,128]{3,1,2,0:T(4,128)S(1)}, u32[]{:S(2)}, u32[]{:S(2)}) %all-to-all-start.6) | async-done | bytes 196640 | tf_op jit(solution)/shard_map/all_to_all | solution.py:43
  333.1 0.9 fusion.28
  (315 shorter events, 76.6 us)
Async XLA Ops:
  2.9 21.5 %collective-permute-start.1 = (f32[2,16,3,128]{3,1,2,0:T(8,128)S(1)}, f32[2,16,3,128]{3,1,2,0:T(8,128)S(1)}, u32[]{:S(2)}, u32[]{:S(2)}) collective-permute-start(f32[2,16,3,128]{3,1,2,0:T(8,128)S(1)} %pad_maximum_fusion.3), channel_id=1, source_target_pairs={{1,0},{2,1},{3,2},{4,3},{5,4},{6,5},{7,6},{8,7},{9,8},{10,9},{11,1... | collective-permute-start | bytes 147464 | tf_op jit(solution)/shard_map/ppermute | solution.py:28
  20.5 16.2 %collective-permute-start = (f32[2,16,3,128]{3,1,2,0:T(8,128)S(1)}, f32[2,16,3,128]{3,1,2,0:T(8,128)S(1)}, u32[]{:S(2)}, u32[]{:S(2)}) collective-permute-start(f32[2,16,3,128]{3,1,2,0:T(8,128)S(1)} %pad_maximum_fusion.3), channel_id=1, source_target_pairs={{0,1},{1,2},{2,3},{3,4},{4,5},{5,6},{6,7},{7,8},{8,9},{9,10},{10,1... | collective-permute-start | bytes 147464 | tf_op jit(solution)/shard_map/ppermute | solution.py:26
  37.8 116.5 %copy-start = (f32[1,16,3,128]{3,1,2,0:T(8,128)S(1)}, f32[1,16,3,128]{3,1,2,0:T(8,128)}, u32[]{:S(2)}) copy-start(f32[1,16,3,128]{3,1,2,0:T(8,128)} %param.12) | copy-start | bytes 73732
  37.8 116.5 %copy-start.1 = (f32[1,16,3,128]{3,1,2,0:T(8,128)S(1)}, f32[1,16,3,128]{3,1,2,0:T(8,128)}, u32[]{:S(2)}) copy-start(f32[1,16,3,128]{3,1,2,0:T(8,128)} %param.13) | copy-start | bytes 73732
  155.1 18.8 %all-to-all-start.1 = ((f32[1,32,192]{2,0,1:T(1,128)}), f32[1,32,192]{2,0,1:T(1,128)S(1)}, u32[]{:S(2)}, u32[]{:S(2)}) async-start(f32[1,32,192]{2,0,1:T(1,128)} %reshape.1027), calls=%async_computation.1 | async-start | bytes 65536 | tf_op jit(solution)/shard_map/all_to_all | solution.py:221
  173.9 16.4 %all-to-all-start = ((f32[1,32,192]{2,0,1:T(1,128)}), f32[1,32,192]{2,0,1:T(1,128)S(1)}, u32[]{:S(2)}, u32[]{:S(2)}) async-start(f32[1,32,192]{2,0,1:T(1,128)} %reshape.1026), calls=%async_computation | async-start | bytes 65536 | tf_op jit(solution)/shard_map/all_to_all | solution.py:215
  190.3 16.4 %all-to-all-start.2 = ((f32[1,32,192]{2,0,1:T(1,128)}), f32[1,32,192]{2,0,1:T(1,128)S(1)}, u32[]{:S(2)}, u32[]{:S(2)}) async-start(f32[1,32,192]{2,0,1:T(1,128)} %reshape.1028), calls=%async_computation.2 | async-start | bytes 65536 | tf_op jit(solution)/shard_map/all_to_all | solution.py:227
  224.3 29.8 %all-to-all-start.5 = ((f32[32,1,16,3,128]{4,2,3,1,0:T(8,128)}), f32[32,1,16,3,128]{4,2,3,1,0:T(8,128)S(1)}, u32[]{:S(2)}, u32[]{:S(2)}) async-start(f32[32,1,16,3,128]{4,2,3,1,0:T(8,128)} %broadcast_in_dim.213), calls=%async_computation.5 | async-start | bytes 1572864 | tf_op jit(solution)/shard_map/all_to_all | solution.py:43
  254.9 20.7 %collective-permute-start.3 = (f32[2,16,3,128]{3,1,2,0:T(8,128)S(1)}, f32[2,16,3,128]{3,1,2,0:T(8,128)S(1)}, u32[]{:S(2)}, u32[]{:S(2)}) collective-permute-start(f32[2,16,3,128]{3,1,2,0:T(8,128)S(1)} %pad_maximum_fusion.2), channel_id=1, source_target_pairs={{1,0},{2,1},{3,2},{4,3},{5,4},{6,5},{7,6},{8,7},{9,8},{10,9},{11,1... | collective-permute-start | bytes 147464 | tf_op jit(solution)/shard_map/ppermute | solution.py:28
  264.4 16.6 %collective-permute-start.2 = (f32[2,16,3,128]{3,1,2,0:T(8,128)S(1)}, f32[2,16,3,128]{3,1,2,0:T(8,128)S(1)}, u32[]{:S(2)}, u32[]{:S(2)}) collective-permute-start(f32[2,16,3,128]{3,1,2,0:T(8,128)S(1)} %pad_maximum_fusion.2), channel_id=1, source_target_pairs={{0,1},{1,2},{2,3},{3,4},{4,5},{5,6},{6,7},{7,8},{8,9},{9,10},{10,1... | collective-permute-start | bytes 147464 | tf_op jit(solution)/shard_map/ppermute | solution.py:26
  267.3 44.5 %all-to-all-start.4 = ((f32[32,1,192]{2,1,0:T(1,128)}), f32[32,1,192]{2,1,0:T(1,128)S(1)}, u32[]{:S(2)}, u32[]{:S(2)}) async-start(f32[32,1,192]{2,1,0:T(1,128)} %copy.51), calls=%async_computation.4 | async-start | bytes 65536 | tf_op jit(solution)/shard_map/all_to_all | solution.py:234
  312.5 20.3 %all-to-all-start.6 = ((f32[32,4,3,128]{3,1,2,0:T(4,128)}), f32[32,4,3,128]{3,1,2,0:T(4,128)S(1)}, u32[]{:S(2)}, u32[]{:S(2)}) async-start(f32[32,4,3,128]{3,1,2,0:T(4,128)} %broadcast_in_dim.214), calls=%async_computation.6 | async-start | bytes 393216 | tf_op jit(solution)/shard_map/all_to_all | solution.py:43
where the time goes:
time: 336 us; the launch traced here: 334 us
  waiting for transfers between devices  82.6 us (25%)
  starting transfers between devices  72.8 us (22%)
  other arithmetic  71.8 us (21%)
  local copies, waits for them, and re-layouts  46.2 us (14%)
  loops' own time  40.4 us (12%)
  blocking collectives  15.9 us (5%)
    mul x20, other arithmetic, pair_force(): weight = weight * left_param[2][:, None] * right_param[2][None, :]  38.2 us
    all_to_all x2, waiting for transfers between devices, sent_to_all(): return lax.all_to_all(copies, axis, split_axis=0, concat_axis=0, tiled=True)  34.1 us
    another operation x1, loops' own time, shards(): lax.map(short_row, jnp.arange(local_beads * domain_cells))  32.4 us
    ppermute x2, starting transfers between devices, with_halo(): lax.ppermute(head, axis, [((i + 1) % count, i) for i in range(count)])  27.2 us
    ppermute x2, waiting for transfers between devices, with_halo(): lax.ppermute(tail, axis, [(i, (i + 1) % count) for i in range(count)])  17.8 us
    all_to_all x1, blocking collectives, shards(): lax.all_to_all(back_position, 'bead', split_axis=0, concat_axis=1, tiled=...  15.9 us
    reduce_sum x20, other arithmetic, pair_force(): radius_sq = jnp.sum(separation * separation, 0)  14.7 us
    reduce_sum x20, other arithmetic, pair_force(): return jnp.sum(weight[None] * separation, 2)  14.3 us
  transfers between devices with their start and end apart: 10, of which 7 were waited for; matrix products, arithmetic and copies ran while one was open for 9% of the time, Pallas kernels for 0%

commit v1 on v0

v1 whole, which is shorter than its diff:
```python
import functools
import math

import jax
import jax.numpy as jnp
import numpy as np
from jax import lax
from jax.experimental import pallas as pl
from jax.experimental.pallas import tpu as pltpu
from jax.sharding import PartitionSpec as P

F32 = jnp.float32
MESH = pl.DeviceIdType.MESH
NB = 32
NS = 16
PC = 8
TIME_STEP = 0.05
INVERSE_TEMP = 32.0
CENTROID_FRICTION = 1.0


def mode_table(n):
    k = np.arange(n)[:, None].astype(np.float64)
    m = np.arange(n)[None, :].astype(np.float64)
    phase = 2.0 * np.pi * k * m / n
    c = np.where(m < n / 2, np.sqrt(2.0 / n) * np.cos(phase), np.sqrt(2.0 / n) * np.sin(phase))
    c = np.where(m == n / 2, np.cos(np.pi * k) / np.sqrt(n), c)
    return np.where(m == 0, 1.0 / np.sqrt(n), c)


def bead_tables():
    c = mode_table(NB)
    n = np.arange(NB)
    freq = 2.0 * (NB / INVERSE_TEMP) * np.sin(np.pi * n / NB)
    gamma = np.where(n == 0, CENTROID_FRICTION, 2.0 * freq)
    c1 = np.exp(-gamma * TIME_STEP)
    kick = np.sqrt((1.0 - c1 * c1) / INVERSE_TEMP)
    cosine = np.cos(freq * TIME_STEP)
    sine = np.sin(freq * TIME_STEP)
    drift = np.where(n == 0, TIME_STEP, sine / np.where(n == 0, 1.0, freq))

    def mix(d):
        return (c * d[None, :]) @ c.T

    pick = np.arange(PC)
    pick = np.where(pick <= PC // 2, pick, pick + NB - PC)
    w = np.sqrt(PC / NB) * mode_table(PC) @ c[:, pick].T
    x_from = (mix(cosine), mix(drift * kick), mix(drift * c1))
    p_from = (mix(-freq * sine), mix(cosine * kick), mix(cosine * c1))
    early_x = np.concatenate([x_from[0], p_from[0], w @ x_from[0]], 0)
    early_n = np.concatenate([x_from[1], p_from[1], w @ x_from[1]], 0)
    late = np.concatenate([x_from[2], p_from[2], w @ x_from[2]], 0)
    table = np.concatenate([early_x, early_n, late], 0).astype(np.float32)
    weights = (w * (0.5 * TIME_STEP * NB / PC)).astype(np.float32)
    return table, weights


def share_bead(cell):
    return (cell // 4) * 8 + 2 + cell % 4


def kernel(own_ref, early_ref, aux_ref, table_ref, w_ref, nx_ref, np_ref,
           ext, xi, acc, eb, kb, late_out, mixed, cont, ret, rb, cb, xs, sacc, fb, xb, zs, zb,
           halo_ss, halo_rs, early_ss, early_rs, late_ss, late_rs, cont_ss, cont_rs, ret_ss, ret_rs,
           xb_ss, xb_rs, zb_ss, zb_rs):
    b = lax.axis_index("bead")
    s = lax.axis_index("space")
    bx = b // 8
    bz8 = b % 8
    up = (s + 1) % NS
    down = (s + NS - 1) % NS
    is_share = (bz8 >= 2) & (bz8 < 6)
    my_cell = bx * 4 + bz8 - 2
    even = s % 2 == 0
    near = jnp.where(even, 2, 0)
    far = jnp.where(even, 0, 2)

    barrier = pltpu.get_barrier_semaphore()

    def greet(i, _):
        other = (b + 1 + i) % NB
        pl.semaphore_signal(barrier, inc=1, device_id={"bead": other, "space": s}, device_id_type=MESH)
        return 0

    pl.semaphore_signal(barrier, inc=1, device_id={"bead": b, "space": up}, device_id_type=MESH)
    pl.semaphore_signal(barrier, inc=1, device_id={"bead": b, "space": down}, device_id_type=MESH)
    lax.fori_loop(0, NB - 1, greet, 0)

    def spread(ref_row):
        return jnp.broadcast_to(ref_row, (128, 128)).T

    def prep(c, _):
        for d in range(4):
            xi[d, c] = spread(own_ref[d, pl.ds(c, 1), :])
        for d in range(3):
            acc[d, c] = jnp.zeros((128, 128), F32)
        return 0

    lax.fori_loop(0, 16, prep, 0)

    def short_pairs(src, base_row, y, y2, shift):
        for z in range(4):
            i = y * 4 + z
            cols = []
            for z2 in range(max(z - 1, 0), min(z + 2, 4)):
                row = y2 * 4 + z2
                xj = src(0, row)
                if shift is not None:
                    xj = xj + shift
                cols.append([jnp.broadcast_to(v, (8, 128)) for v in (xj, src(1, row), src(2, row), src(3, row), src(4, row))])
            for t in range(16):
                lanes = pl.ds(8 * t, 8)
                xa, ya, za, sa = (xi[d, i, lanes, :] for d in range(4))
                tot = [acc[d, i, lanes, :] for d in range(3)]
                for xj, yj, zj, sj, ej in cols:
                    dx = xa - xj
                    dy = ya - yj
                    dz = za - zj
                    r2 = dx * dx + dy * dy + dz * dz
                    sp = sa + sj
                    s2 = sp * sp
                    p = 1.0 / (r2 + s2)
                    m = jnp.maximum(1.0 - r2, 0.0)
                    q = s2 * p
                    w = q * q * q
                    pm = p * m
                    bb = pm + (2.0 / 3.0)
                    g = (w * m) * (w * (pm + bb) - bb) * ej
                    tot = [tot[0] + g * dx, tot[1] + g * dy, tot[2] + g * dz]
                for d in range(3):
                    acc[d, i, lanes, :] = tot[d]

    def own_src(d, row):
        return own_ref[d, pl.ds(row, 1), :]

    def own_row(n, _):
        y = n // 3
        y2 = y + n % 3 - 1

        @pl.when((y2 >= 0) & (y2 < 4))
        def _():
            short_pairs(own_src, None, y, y2, None)
        return 0

    lax.fori_loop(0, 7, own_row, 0)

    pl.semaphore_wait(barrier, NB + 1)

    halo_up = pltpu.make_async_remote_copy(
        src_ref=own_ref, dst_ref=ext.at[0], send_sem=halo_ss.at[0], recv_sem=halo_rs.at[0],
        device_id={"bead": b, "space": up}, device_id_type=MESH)
    halo_down = pltpu.make_async_remote_copy(
        src_ref=own_ref, dst_ref=ext.at[1], send_sem=halo_ss.at[1], recv_sem=halo_rs.at[1],
        device_id={"bead": b, "space": down}, device_id_type=MESH)
    halo_up.start()
    halo_down.start()

    def to_share(src, dst, ss, rs, c):
        target = share_bead(c)

        @pl.when(target != b)
        def _():
            pltpu.make_async_remote_copy(
                src_ref=src.at[c], dst_ref=dst.at[b], send_sem=ss.at[c], recv_sem=rs,
                device_id={"bead": target, "space": s}, device_id_type=MESH).start()

        @pl.when(target == b)
        def _():
            pltpu.make_async_copy(src.at[c], dst.at[b], rs).start()

    def sent_share(src, dst, ss, rs, c):
        target = share_bead(c)

        @pl.when(target != b)
        def _():
            pltpu.make_async_remote_copy(
                src_ref=src.at[c], dst_ref=dst.at[b], send_sem=ss.at[c], recv_sem=rs,
                device_id={"bead": target, "space": s}, device_id_type=MESH).wait_send()

    def send_early(c, _):
        to_share(early_ref, eb, early_ss, early_rs, c)
        return 0

    lax.fori_loop(0, 16, send_early, 0)
    lax.fori_loop(7, 12, own_row, 0)

    def ext_src(k):
        return lambda d, row: ext[k, d, pl.ds(row, 1), :]

    def wait_halo(side):
        pltpu.make_async_remote_copy(
            src_ref=own_ref, dst_ref=ext.at[side], send_sem=halo_ss.at[side], recv_sem=halo_rs.at[side],
            device_id={"bead": b, "space": up}, device_id_type=MESH).wait_recv()

    def both(which):
        side = jnp.where(even, 1 - which, which)
        shift = jnp.where(side == 1, 2.0, -2.0)
        return side, shift

    near_side, near_shift = both(0)
    far_side, far_shift = both(1)

    wait_halo(near_side)

    def near_row(n, _):
        y = n // 3
        y2 = y + n % 3 - 1

        @pl.when((y2 >= 0) & (y2 < 4))
        def _():
            short_pairs(ext_src(near_side), None, y, y2, near_shift)
        return 0

    lax.fori_loop(0, 12, near_row, 0)

    def mm(a, v):
        return jnp.dot(a, v, preferred_element_type=F32, precision=lax.Precision.HIGHEST)

    @pl.when(is_share)
    def _():
        pltpu.make_async_copy(eb, eb, early_rs).wait()
        for d in range(3):
            mixed[d] = mm(table_ref[0:72, :], eb[:, d, :]) + mm(table_ref[72:144, :], eb[:, 3 + d, :])

    wait_halo(far_side)

    def far_y(y, _):
        def far_row(n, _):
            y2 = y + n - 1

            @pl.when((y2 >= 0) & (y2 < 4))
            def _():
                short_pairs(ext_src(far_side), None, y, y2, far_shift)
            return 0

        lax.fori_loop(0, 3, far_row, 0)
        for z in range(4):
            c = y * 4 + z
            rows = [jnp.sum(acc[d, c].T, 0, keepdims=True) for d in range(3)]
            late_out[c] = aux_ref[c, 0:3, :] + aux_ref[c, 3:4, :] * jnp.concatenate(rows, 0)
        for z in range(4):
            to_share(late_out, kb, late_ss, late_rs, y * 4 + z)
        return 0

    lax.fori_loop(0, 4, far_y, 0)

    def cont_target(n):
        r = n // 12
        q = n % 12 // 3
        e = n % 3
        by = q // 2
        bz = q % 2
        jy = my_cell // 4 - by
        jz = my_cell % 4 - bz
        ok = is_share & (jy >= 0) & (jy < 3) & (jz >= 0) & (jz < 3)
        tb = (r % 4) * 8 + (r // 4) * 4 + q
        ts = (s + e + NS - 1) % NS
        slot = 2 - e
        return ok, r, tb, ts, slot, jy, jz, e

    def cont_copy(n):
        ok, r, tb, ts, slot, jy, jz, e = cont_target(n)
        remote = pltpu.make_async_remote_copy(
            src_ref=cont.at[r], dst_ref=cb.at[slot, jy, jz], send_sem=cont_ss.at[n], recv_sem=cont_rs.at[slot],
            device_id={"bead": tb, "space": ts}, device_id_type=MESH)
        local = pltpu.make_async_copy(cont.at[r], cb.at[slot, jy, jz], cont_rs.at[slot])
        mine = (tb == b) & (e == 1)
        return ok, mine, remote, local

    @pl.when(is_share)
    def _():
        pltpu.make_async_copy(kb, kb, late_rs).wait()
        for d in range(3):
            cont[:, d, :] = mixed[d, 64:72, :] + mm(table_ref[208:216, :], kb[:, d, :])

        def send_cont(n, _):
            ok, mine, remote, local = cont_copy(n)

            @pl.when(ok & jnp.logical_not(mine))
            def _():
                remote.start()

            @pl.when(ok & mine)
            def _():
                local.start()
            return 0

        lax.fori_loop(0, 96, send_cont, 0)
        for d in range(3):
            full = mixed[d, 0:64, :] + mm(table_ref[144:208, :], kb[:, d, :])
            ret[:, d, :] = full[0:32]
            ret[:, 3 + d, :] = full[32:64]

        def send_ret(k, _):
            @pl.when(k != b)
            def _():
                pltpu.make_async_remote_copy(
                    src_ref=ret.at[k], dst_ref=rb.at[my_cell], send_sem=ret_ss.at[k], recv_sem=ret_rs,
                    device_id={"bead": k, "space": s}, device_id_type=MESH).start()

            @pl.when(k == b)
            def _():
                pltpu.make_async_copy(ret.at[k], rb.at[my_cell], ret_rs).start()
            return 0

        lax.fori_loop(0, NB, send_ret, 0)

    rhi = bz8 // 4
    q = bz8 % 4
    by = q // 2
    bz = q % 2
    flip = lambda bit, v, top: jnp.where(bit == 1, top - v, v)

    def wait_cont(slot):
        pltpu.make_async_copy(cb.at[slot], cb.at[slot], cont_rs.at[slot]).wait()

    wait_cont(1)
    for iy in range(2):
        for iz in range(2):
            wy = by + iy
            wz = bz + iz
            me = cb[1, wy, wz]
            cell = (2 * by + iy) * 4 + 2 * bz + iz
            xs[0, iy, iz] = spread(2.0 * me[0:1])
            xs[1, iy, iz] = spread(2.0 * (me[1:2] + wy.astype(F32)))
            xs[2, iy, iz] = spread(2.0 * (me[2:3] + wz.astype(F32)))
            xs[3, iy, iz] = spread(own_ref[3, pl.ds(cell, 1), :])
            for d in range(3):
                sacc[d, iy, iz] = jnp.zeros((128, 128), F32)

    Y_PAIRS = ((0, 0), (0, 1), (1, 0), (1, 1), (1, 2))

    def slow_pairs(slot, params, shift):
        def one(n, _):
            fy = jnp.where(n < 2, 0, 1)
            jy = flip(by, jnp.where(n < 2, n, n - 2), 2)
            iy = flip(by, fy, 1)
            js = []
            for jz0 in range(3):
                jz = flip(bz, jz0, 2)
                v = cb[slot, jy, jz]
                row = (by + jy) * 4 + bz + jz
                vals = (2.0 * v[0:1] + shift, 2.0 * (v[1:2] + jy.astype(F32)), 2.0 * (v[2:3] + jz.astype(F32)), params(3, row), params(4, row))
                js.append([jnp.broadcast_to(a, (8, 128)) for a in vals])
            for iz0 in range(2):
                iz = flip(bz, iz0, 1)
                for t in range(16):
                    lanes = pl.ds(8 * t, 8)
                    xa, ya, za, sa = (xs[d, iy, iz, lanes, :] for d in range(4))
                    tot = [sacc[d, iy, iz, lanes, :] for d in range(3)]
                    for jz0 in (range(2) if iz0 == 0 else range(3)):
                        xj, yj, zj, sj, ej = js[jz0]
                        dx = xa - xj
                        dy = ya - yj
                        dz = za - zj
                        r2 = dx * dx + dy * dy + dz * dz
                        sp = sa + sj
                        s2 = sp * sp
                        p = 1.0 / (r2 + s2)
                        m2 = jnp.maximum(1.0 - r2, 0.0)
                        m1 = jnp.maximum(1.0 - 0.25 * r2, 0.0)
                        w = s2 * p
                        w = w * w * w
                        ps = p * (m1 * m1 - m2 * m2)
                        bb = ps + (m1 * (1.0 / 6.0) - m2 * (2.0 / 3.0))
                        g = w * (w * (ps + bb) - bb) * ej
                        tot = [tot[0] + g * dx, tot[1] + g * dy, tot[2] + g * dz]
                    for d in range(3):
                        sacc[d, iy, iz, lanes, :] = tot[d]
            return 0

        lax.fori_loop(0, 5, one, 0)

    slow_pairs(1, own_src, 0.0)
    near_slot = near_side * 2
    far_slot = far_side * 2
    wait_cont(near_slot)
    slow_pairs(near_slot, ext_src(near_side), near_shift)
    wait_cont(far_slot)
    slow_pairs(far_slot, ext_src(far_side), far_shift)

    for iy in range(2):
        for iz in range(2):
            cell = (2 * by + iy) * 4 + 2 * bz + iz
            rows = [jnp.sum(sacc[d, iy, iz].T, 0, keepdims=True) for d in range(3)]
            fb[2 * iy + iz] = aux_ref[cell, 4:5, :] * jnp.concatenate(rows, 0)

    def x_copy(i):
        other = (bx + 1 + i) % 4
        return pltpu.make_async_remote_copy(
            src_ref=fb, dst_ref=xb.at[bx], send_sem=xb_ss.at[i], recv_sem=xb_rs,
            device_id={"bead": other * 8 + bz8, "space": s}, device_id_type=MESH)

    for i in range(3):
        x_copy(i).start()
    pltpu.make_async_copy(fb, xb.at[bx], xb_rs).start()
    pltpu.make_async_copy(xb, xb, xb_rs).wait()

    def z_copy(i):
        other = (bz8 + i) % 8
        return pltpu.make_async_remote_copy(
            src_ref=zs.at[i], dst_ref=zb.at[bz8], send_sem=zb_ss.at[i], recv_sem=zb_rs,
            device_id={"bead": bx * 8 + other, "space": s}, device_id_type=MESH)

    for i in range(8):
        k = bx * 8 + (bz8 + i) % 8
        part = w_ref[rhi * 4, k] * xb[0]
        for x2 in range(1, 4):
            part = part + w_ref[rhi * 4 + x2, k] * xb[x2]
        zs[i] = part
    for i in range(1, 8):
        z_copy(i).start()
    pltpu.make_async_copy(zs.at[0], zb.at[bz8], zb_rs).start()

    pltpu.make_async_copy(rb, rb, ret_rs).wait()
    for c in range(16):
        nx_ref[c] = rb[c, 0:3, :]
    pltpu.make_async_copy(zb, zb, zb_rs).wait()
    for c in range(16):
        y, z = c // 4, c % 4
        blk = (y // 2) * 2 + z // 2
        at = (y % 2) * 2 + z % 2
        np_ref[c] = rb[c, 3:6, :] * aux_ref[c, 5:6, :] + (zb[blk, at] + zb[4 + blk, at])

    halo_up.wait_send()
    halo_down.wait_send()

    def drain(c, _):
        sent_share(early_ref, eb, early_ss, early_rs, c)
        sent_share(late_out, kb, late_ss, late_rs, c)
        return 0

    lax.fori_loop(0, 16, drain, 0)

    @pl.when(is_share)
    def _():
        def drain_cont(n, _):
            ok, mine, remote, local = cont_copy(n)

            @pl.when(ok & jnp.logical_not(mine))
            def _():
                remote.wait_send()
            return 0

        lax.fori_loop(0, 96, drain_cont, 0)

        def drain_ret(k, _):
            @pl.when(k != b)
            def _():
                pltpu.make_async_remote_copy(
                    src_ref=ret.at[k], dst_ref=rb.at[my_cell], send_sem=ret_ss.at[k], recv_sem=ret_rs,
                    device_id={"bead": k, "space": s}, device_id_type=MESH).wait_send()
            return 0

        lax.fori_loop(0, NB, drain_ret, 0)

    for i in range(3):
        x_copy(i).wait_send()
    for i in range(1, 8):
        z_copy(i).wait_send()


def shards(positions, momenta, noise, atom_types, occupancy, type_sigma, type_eps, type_mass):
    table, weights = bead_tables()
    hot = atom_types[..., None] == jnp.arange(4)
    pick = lambda v: jnp.sum(jnp.where(hot, v, 0.0), -1)
    sigma = pick(type_sigma)
    mass = pick(type_mass)
    live = (jnp.arange(128)[None, :] < occupancy[:, None]).astype(F32)
    e = jnp.sqrt(pick(type_eps)) * live
    l = np.arange(16)
    corner = np.stack([np.full(16, -0.5), l // 4 - 2.0, l % 4 - 2.0], 0).astype(np.float32)
    x = positions[0]
    scaled = 2.0 * (jnp.transpose(x, (1, 0, 2)) + corner[:, :, None])
    own = jnp.concatenate([scaled, sigma[None], e[None]], 0)
    early = jnp.concatenate([x, noise[0] / jnp.sqrt(mass)[:, None, :]], 1)
    zero = jnp.zeros_like(e)
    coeff = (0.5 * TIME_STEP * 48.0) * e / mass
    aux = jnp.concatenate(
        [momenta[0] / mass[:, None, :], jnp.stack([coeff, 48.0 * e, mass, zero, zero], 1)], 1)
    vm = pl.BlockSpec(memory_space=pltpu.VMEM)
    out = jax.ShapeDtypeStruct((16, 3, 128), F32)
    V = lambda *shape: pltpu.VMEM(shape, F32)
    D = pltpu.SemaphoreType.DMA
    nx, pn = pl.pallas_call(
        kernel,
        out_shape=(out, out),
        in_specs=[vm, vm, vm, vm, pl.BlockSpec(memory_space=pltpu.SMEM)],
        out_specs=(vm, vm),
        scratch_shapes=[
            V(2, 5, 16, 128), V(4, 16, 128, 128), V(3, 16, 128, 128), V(32, 6, 128), V(32, 3, 128),
            V(16, 3, 128), V(3, 72, 128), V(8, 3, 128), V(32, 6, 128), V(16, 6, 128), V(3, 3, 3, 3, 128),
            V(4, 2, 2, 128, 128), V(3, 2, 2, 128, 128), V(4, 3, 128), V(4, 4, 3, 128), V(8, 4, 3, 128), V(8, 4, 3, 128),
            D((2,)), D((2,)), D((16,)), D, D((16,)), D, D((96,)), D((3,)), D((32,)), D, D((3,)), D, D((8,)), D,
        ],
        compiler_params=pltpu.CompilerParams(collective_id=0, has_side_effects=True, vmem_limit_bytes=40 << 20),
    )(own, early, aux, jnp.asarray(table), jnp.asarray(weights))
    return nx[None], pn[None]


def solution(mesh):
    full = P("bead", "space", None, None)
    placed = (full, full, full, P("space", None), P("space"), P(), P(), P())
    return jax.shard_map(shards, mesh=mesh, in_specs=placed, out_specs=(full, full), check_vma=False)
```

time: 336 us -> 78.8 us (0.23)
  the two profiles are of different devices: /device:TPU:6 before, /device:TPU:64 now
where the time goes in v1:
time: 78.8 us; the launch traced here: 78.4 us
  Pallas kernels  71.7 us (91%)
  local copies, waits for them, and re-layouts  4.81 us (6%)
  other arithmetic  1.12 us (1%)
    pallas_call x1, Pallas kernels, shards(): pl.pallas_call(kernel, out_shape=(out, out), in_specs=[vm, vm, vm, vm, pl...  71.7 us
    unnamed x17, local copies, waits for them, and re-layouts  4.71 us

profile of v1, /device:TPU:64, one launch (start us, length us, event | category | flops | bytes accessed | tf_op | source)
XLA Modules:
  0.0 78.4 jit_solution(2852392573044919788)
XLA Ops:
  0.6 0.8 select_reduce_fusion
  1.4 0.0 copy-start.6
  1.4 0.6 copy-done.6
  2.1 0.1 bitcast_select_fusion
  2.2 0.0 copy-start.3
  2.2 0.1 broadcast_multiply_fusion
  2.3 0.6 copy-done.3
  2.9 0.0 copy-start.4
  2.9 0.7 copy-done.4
  3.7 0.0 copy-start.2
  3.7 0.0 copy-start.5
  3.7 0.1 concatenate.15.aux_ref
  3.8 0.6 copy-done.2
  4.4 0.0 copy-done.5
  4.4 0.1 fusion.1
  4.6 0.0 copy-start
  4.6 0.0 copy-start.1
  4.6 0.8 %copy-done = f32[216,32]{1,0:T(8,128)S(1)} copy-done((f32[216,32]{1,0:T(8,128)S(1)}, f32[216,32]{1,0:T(8,128)}, u32[]{:S(2)}) %copy-start) | copy-done | bytes 27672
  5.5 0.0 copy-done.1
  5.5 71.7 %shard_map.122 = (f32[16,3,128]{2,1,0:T(4,128)S(1)}, f32[16,3,128]{2,1,0:T(4,128)S(1)}) custom-call(f32[5,16,128]{2,1,0:T(8,128)S(1)} %copy.24.own_ref, f32[16,6,128]{2,1,0:T(8,128)S(1)} %pad_maximum_fusion.1.early_ref, f32[16,8,128]{2,1,0:T(8,128)S(1)} %concatenate.15.aux_ref, f32[216,32]{1,0:T(8,128)S(1)} %copy-done, f32[8,32]{1,0:T(8,128)S(1)} %copy-done.1), custom_call_target="tpu_custom_call" | custom-call | tf_op jit(solution)/shard_map/pallas_call | solution.py:485
  77.2 0.6 copy.25
  77.8 0.6 copy.26
  (10 shorter events, 0.1 us)
Async XLA Ops:
  1.4 0.7 copy-start.6
  2.2 0.7 copy-start.3
  2.9 0.7 copy-start.4
  3.7 0.7 copy-start.2
  3.7 0.7 copy-start.5
  4.6 0.9 %copy-start = (f32[216,32]{1,0:T(8,128)S(1)}, f32[216,32]{1,0:T(8,128)}, u32[]{:S(2)}) copy-start(f32[216,32]{1,0:T(8,128)} %constant.17.clone.table_ref) | copy-start | bytes 82948
  4.6 0.9 %copy-start.1 = (f32[8,32]{1,0:T(8,128)S(1)}, f32[8,32]{1,0:T(8,128)}, u32[]{:S(2)}) copy-start(f32[8,32]{1,0:T(8,128)} %constant.18.clone.w_ref) | copy-start | bytes 3076

commit v2 on v1

--- a/solution.py
+++ b/solution.py
@@ -59,9 +59,11 @@
     return (cell // 4) * 8 + 2 + cell % 4
 
 
-def kernel(own_ref, early_ref, aux_ref, table_ref, w_ref, nx_ref, np_ref,
+def kernel(pos_in, mom_in, noise_in, types_in, occ_in, sig_in, eps_in, mass_in, table_in, w_in, nx_ref, np_ref,
+           pos, mom, noise, types, table_ref, occ, ts_sig, ts_eps, ts_mass, w_ref,
+           own_ref, early_ref, pm, invm, kcoef, e48, mass, slots,
            ext, xi, acc, eb, kb, late_out, mixed, cont, ret, rb, cb, xs, sacc, fb, xb, zs, zb,
-           halo_ss, halo_rs, early_ss, early_rs, late_ss, late_rs, cont_ss, cont_rs, ret_ss, ret_rs,
+           in_s, halo_ss, halo_rs, early_ss, early_rs, late_ss, late_rs, cont_ss, cont_own_ss, cont_rs, ret_ss, ret_rs,
            xb_ss, xb_rs, zb_ss, zb_rs):
     b = lax.axis_index("bead")
     s = lax.axis_index("space")
@@ -72,8 +74,6 @@
     is_share = (bz8 >= 2) & (bz8 < 6)
     my_cell = bx * 4 + bz8 - 2
     even = s % 2 == 0
-    near = jnp.where(even, 2, 0)
-    far = jnp.where(even, 0, 2)
 
     barrier = pltpu.get_barrier_semaphore()
 
@@ -85,6 +85,44 @@
     pl.semaphore_signal(barrier, inc=1, device_id={"bead": b, "space": up}, device_id_type=MESH)
     pl.semaphore_signal(barrier, inc=1, device_id={"bead": b, "space": down}, device_id_type=MESH)
     lax.fori_loop(0, NB - 1, greet, 0)
+
+    loads = [
+        pltpu.make_async_copy(src, dst, in_s.at[i])
+        for i, (src, dst) in enumerate((
+            (occ_in, occ), (sig_in, ts_sig), (eps_in, ts_eps), (mass_in, ts_mass), (types_in, types),
+            (pos_in, pos), (mom_in, mom), (noise_in, noise), (table_in, table_ref), (w_in, w_ref)))
+    ]
+    for load in loads:
+        load.start()
+    for load in loads:
+        load.wait()
+
+    kind = types[...]
+
+    def pick(tab):
+        v = jnp.where(kind == 0, tab[0], tab[1])
+        v = jnp.where(kind == 2, tab[2], v)
+        return jnp.where(kind == 3, tab[3], v)
+
+    m_all = pick(ts_mass)
+    inv = 1.0 / m_all
+    slot_index = lax.broadcasted_iota(jnp.int32, (1, 128), 1)
+    live = jnp.concatenate([jnp.where(slot_index < occ[c], 1.0, 0.0) for c in range(16)], 0)
+    e_all = jnp.sqrt(pick(ts_eps)) * live
+    mass[...] = m_all
+    invm[...] = inv
+    e48[...] = 48.0 * e_all
+    kcoef[...] = (0.5 * TIME_STEP * 48.0) * e_all * inv
+    root = jnp.sqrt(inv)
+    cell_of = lax.broadcasted_iota(jnp.int32, (16, 128), 0)
+    corner = (-0.5, (cell_of // 4).astype(F32) - 2.0, (cell_of % 4).astype(F32) - 2.0)
+    for d in range(3):
+        own_ref[d] = 2.0 * (pos[0, d] + corner[d])
+        early_ref[:, d, :] = pos[0, d]
+        early_ref[:, 3 + d, :] = noise[0, d] * root
+        pm[:, d, :] = mom[0, d] * inv
+    own_ref[3] = pick(ts_sig)
+    own_ref[4] = e_all
 
     def spread(ref_row):
         return jnp.broadcast_to(ref_row, (128, 128)).T
@@ -161,21 +199,21 @@
         @pl.when(target != b)
         def _():
             pltpu.make_async_remote_copy(
-                src_ref=src.at[c], dst_ref=dst.at[b], send_sem=ss.at[c], recv_sem=rs,
+                src_ref=src.at[c], dst_ref=dst.at[b], send_sem=ss, recv_sem=rs,
                 device_id={"bead": target, "space": s}, device_id_type=MESH).start()
 
         @pl.when(target == b)
         def _():
             pltpu.make_async_copy(src.at[c], dst.at[b], rs).start()
 
-    def sent_share(src, dst, ss, rs, c):
-        target = share_bead(c)
-
-        @pl.when(target != b)
-        def _():
-            pltpu.make_async_remote_copy(
-                src_ref=src.at[c], dst_ref=dst.at[b], send_sem=ss.at[c], recv_sem=rs,
-                device_id={"bead": target, "space": s}, device_id_type=MESH).wait_send()
+    def sent_share(src, ss):
+        @pl.when(is_share)
+        def _():
+            pltpu.make_async_copy(src.at[pl.ds(0, 15)], src.at[pl.ds(0, 15)], ss).wait()
+
+        @pl.when(jnp.logical_not(is_share))
+        def _():
+            pltpu.make_async_copy(src, src, ss).wait()
 
     def send_early(c, _):
         to_share(early_ref, eb, early_ss, early_rs, c)
@@ -222,6 +260,9 @@
         for d in range(3):
             mixed[d] = mm(table_ref[0:72, :], eb[:, d, :]) + mm(table_ref[72:144, :], eb[:, 3 + d, :])
 
+    halo_up.wait_send()
+    halo_down.wait_send()
+    sent_share(early_ref, early_ss)
     wait_halo(far_side)
 
     def far_y(y, _):
@@ -237,35 +278,35 @@
         for z in range(4):
             c = y * 4 + z
             rows = [jnp.sum(acc[d, c].T, 0, keepdims=True) for d in range(3)]
-            late_out[c] = aux_ref[c, 0:3, :] + aux_ref[c, 3:4, :] * jnp.concatenate(rows, 0)
+            late_out[c] = pm[c] + kcoef[pl.ds(c, 1), :] * jnp.concatenate(rows, 0)
         for z in range(4):
             to_share(late_out, kb, late_ss, late_rs, y * 4 + z)
         return 0
 
     lax.fori_loop(0, 4, far_y, 0)
 
-    def cont_target(n):
-        r = n // 12
-        q = n % 12 // 3
-        e = n % 3
-        by = q // 2
-        bz = q % 2
-        jy = my_cell // 4 - by
-        jz = my_cell % 4 - bz
-        ok = is_share & (jy >= 0) & (jy < 3) & (jz >= 0) & (jz < 3)
-        tb = (r % 4) * 8 + (r // 4) * 4 + q
-        ts = (s + e + NS - 1) % NS
-        slot = 2 - e
-        return ok, r, tb, ts, slot, jy, jz, e
-
-    def cont_copy(n):
-        ok, r, tb, ts, slot, jy, jz, e = cont_target(n)
-        remote = pltpu.make_async_remote_copy(
-            src_ref=cont.at[r], dst_ref=cb.at[slot, jy, jz], send_sem=cont_ss.at[n], recv_sem=cont_rs.at[slot],
-            device_id={"bead": tb, "space": ts}, device_id_type=MESH)
-        local = pltpu.make_async_copy(cont.at[r], cb.at[slot, jy, jz], cont_rs.at[slot])
-        mine = (tb == b) & (e == 1)
-        return ok, mine, remote, local
+    my_y = my_cell // 4
+    my_z = my_cell % 4
+    y_first, y_last = jnp.where(my_y == 3, 1, 0), jnp.where(my_y == 0, 1, 2)
+    z_first, z_last = jnp.where(my_z == 3, 1, 0), jnp.where(my_z == 0, 1, 2)
+    blocks = (y_last - y_first) * (z_last - z_first)
+    far_space = jnp.where(even, down, up)
+    near_space = jnp.where(even, up, down)
+    far_dst = jnp.where(even, 2, 0)
+    near_dst = jnp.where(even, 0, 2)
+    my_r = (bz8 // 4) * 4 + bx
+    has_own = is_share & (my_y - (bz8 % 4) // 2 >= 0) & (my_y - (bz8 % 4) // 2 < 3) & (
+        my_z - bz8 % 2 >= 0) & (my_z - bz8 % 2 < 3)
+
+    def over_blocks(body):
+        def outer(by, _):
+            def inner(bz, _):
+                body(by * 2 + bz, my_y - by, my_z - bz)
+                return 0
+
+            return lax.fori_loop(z_first, z_last, inner, 0)
+
+        lax.fori_loop(y_first, y_last, outer, 0)
 
     @pl.when(is_share)
     def _():
@@ -273,19 +314,32 @@
         for d in range(3):
             cont[:, d, :] = mixed[d, 64:72, :] + mm(table_ref[208:216, :], kb[:, d, :])
 
-        def send_cont(n, _):
-            ok, mine, remote, local = cont_copy(n)
-
-            @pl.when(ok & jnp.logical_not(mine))
-            def _():
-                remote.start()
-
-            @pl.when(ok & mine)
-            def _():
-                local.start()
-            return 0
-
-        lax.fori_loop(0, 96, send_cont, 0)
+        def outside(space, slot):
+            def body(q, jy, jz):
+                for r in range(PC):
+                    pltpu.make_async_remote_copy(
+                        src_ref=cont.at[r], dst_ref=cb.at[slot, jy, jz], send_sem=cont_ss, recv_sem=cont_rs.at[slot],
+                        device_id={"bead": (r % 4) * 8 + (r // 4) * 4 + q, "space": space}, device_id_type=MESH).start()
+            over_blocks(body)
+
+        outside(far_space, far_dst)
+        outside(near_space, near_dst)
+
+        def inside(q, jy, jz):
+            for r in range(PC):
+                tb = (r % 4) * 8 + (r // 4) * 4 + q
+
+                @pl.when(tb != b)
+                def _():
+                    pltpu.make_async_remote_copy(
+                        src_ref=cont.at[r], dst_ref=cb.at[1, jy, jz], send_sem=cont_own_ss, recv_sem=cont_rs.at[1],
+                        device_id={"bead": tb, "space": s}, device_id_type=MESH).start()
+
+                @pl.when(tb == b)
+                def _():
+                    pltpu.make_async_copy(cont.at[r], cb.at[1, jy, jz], cont_rs.at[1]).start()
+
+        over_blocks(inside)
         for d in range(3):
             full = mixed[d, 0:64, :] + mm(table_ref[144:208, :], kb[:, d, :])
             ret[:, d, :] = full[0:32]
@@ -295,7 +349,7 @@
             @pl.when(k != b)
             def _():
                 pltpu.make_async_remote_copy(
-                    src_ref=ret.at[k], dst_ref=rb.at[my_cell], send_sem=ret_ss.at[k], recv_sem=ret_rs,
+                    src_ref=ret.at[k], dst_ref=rb.at[my_cell], send_sem=ret_ss, recv_sem=ret_rs,
                     device_id={"bead": k, "space": s}, device_id_type=MESH).start()
 
             @pl.when(k == b)
@@ -383,7 +437,7 @@
         for iz in range(2):
             cell = (2 * by + iy) * 4 + 2 * bz + iz
             rows = [jnp.sum(sacc[d, iy, iz].T, 0, keepdims=True) for d in range(3)]
-            fb[2 * iy + iz] = aux_ref[cell, 4:5, :] * jnp.concatenate(rows, 0)
+            fb[2 * iy + iz] = e48[pl.ds(cell, 1), :] * jnp.concatenate(rows, 0)
 
     def x_copy(i):
         other = (bx + 1 + i) % 4
@@ -394,6 +448,32 @@
     for i in range(3):
         x_copy(i).start()
     pltpu.make_async_copy(fb, xb.at[bx], xb_rs).start()
+    pltpu.make_async_copy(rb, rb, ret_rs).wait()
+    for d in range(3):
+        nx_ref[0, d] = rb[:, d, :]
+        np_ref[0, d] = rb[:, 3 + d, :] * mass[...]
+    sent_share(late_out, late_ss)
+
+    def wait_slots(sem, n):
+        pltpu.make_async_copy(slots.at[pl.ds(0, n)], slots.at[pl.ds(0, n)], sem).wait()
+
+    for nq in (1, 2, 4):
+        @pl.when(is_share & (blocks == nq))
+        def _():
+            wait_slots(cont_ss, 16 * nq)
+
+        @pl.when(is_share & (blocks == nq) & has_own)
+        def _():
+            wait_slots(cont_own_ss, 8 * nq - 1)
+
+        @pl.when(is_share & (blocks == nq) & jnp.logical_not(has_own))
+        def _():
+            wait_slots(cont_own_ss, 8 * nq)
+
+    @pl.when(is_share)
+    def _():
+        pltpu.make_async_copy(ret.at[pl.ds(0, NB - 1)], ret.at[pl.ds(0, NB - 1)], ret_ss).wait()
+
     pltpu.make_async_copy(xb, xb, xb_rs).wait()
 
     def z_copy(i):
@@ -412,48 +492,14 @@
         z_copy(i).start()
     pltpu.make_async_copy(zs.at[0], zb.at[bz8], zb_rs).start()
 
-    pltpu.make_async_copy(rb, rb, ret_rs).wait()
+    pltpu.make_async_copy(zb, zb, zb_rs).wait()
+    slow = []
     for c in range(16):
-        nx_ref[c] = rb[c, 0:3, :]
-    pltpu.make_async_copy(zb, zb, zb_rs).wait()
-    for c in range(16):
-        y, z = c // 4, c % 4
-        blk = (y // 2) * 2 + z // 2
-        at = (y % 2) * 2 + z % 2
-        np_ref[c] = rb[c, 3:6, :] * aux_ref[c, 5:6, :] + (zb[blk, at] + zb[4 + blk, at])
-
-    halo_up.wait_send()
-    halo_down.wait_send()
-
-    def drain(c, _):
-        sent_share(early_ref, eb, early_ss, early_rs, c)
-        sent_share(late_out, kb, late_ss, late_rs, c)
-        return 0
-
-    lax.fori_loop(0, 16, drain, 0)
-
-    @pl.when(is_share)
-    def _():
-        def drain_cont(n, _):
-            ok, mine, remote, local = cont_copy(n)
-
-            @pl.when(ok & jnp.logical_not(mine))
-            def _():
-                remote.wait_send()
-            return 0
-
-        lax.fori_loop(0, 96, drain_cont, 0)
-
-        def drain_ret(k, _):
-            @pl.when(k != b)
-            def _():
-                pltpu.make_async_remote_copy(
-                    src_ref=ret.at[k], dst_ref=rb.at[my_cell], send_sem=ret_ss.at[k], recv_sem=ret_rs,
-                    device_id={"bead": k, "space": s}, device_id_type=MESH).wait_send()
-            return 0
-
-        lax.fori_loop(0, NB, drain_ret, 0)
-
+        blk = (c // 8) * 2 + (c % 4) // 2
+        at = (c // 4 % 2) * 2 + c % 2
+        slow.append(zb[blk, at] + zb[4 + blk, at])
+    for d in range(3):
+        np_ref[0, d] = np_ref[0, d] + jnp.concatenate([v[d:d + 1] for v in slow], 0)
     for i in range(3):
         x_copy(i).wait_send()
     for i in range(1, 8):
@@ -462,40 +508,31 @@
 
 def shards(positions, momenta, noise, atom_types, occupancy, type_sigma, type_eps, type_mass):
     table, weights = bead_tables()
-    hot = atom_types[..., None] == jnp.arange(4)
-    pick = lambda v: jnp.sum(jnp.where(hot, v, 0.0), -1)
-    sigma = pick(type_sigma)
-    mass = pick(type_mass)
-    live = (jnp.arange(128)[None, :] < occupancy[:, None]).astype(F32)
-    e = jnp.sqrt(pick(type_eps)) * live
-    l = np.arange(16)
-    corner = np.stack([np.full(16, -0.5), l // 4 - 2.0, l % 4 - 2.0], 0).astype(np.float32)
-    x = positions[0]
-    scaled = 2.0 * (jnp.transpose(x, (1, 0, 2)) + corner[:, :, None])
-    own = jnp.concatenate([scaled, sigma[None], e[None]], 0)
-    early = jnp.concatenate([x, noise[0] / jnp.sqrt(mass)[:, None, :]], 1)
-    zero = jnp.zeros_like(e)
-    coeff = (0.5 * TIME_STEP * 48.0) * e / mass
-    aux = jnp.concatenate(
-        [momenta[0] / mass[:, None, :], jnp.stack([coeff, 48.0 * e, mass, zero, zero], 1)], 1)
+    anywhere = pl.BlockSpec(memory_space=pltpu.HBM)
     vm = pl.BlockSpec(memory_space=pltpu.VMEM)
-    out = jax.ShapeDtypeStruct((16, 3, 128), F32)
+    out = jax.ShapeDtypeStruct((1, 3, 16, 128), F32)
     V = lambda *shape: pltpu.VMEM(shape, F32)
+    S = lambda shape, kind: pltpu.SMEM(shape, kind)
     D = pltpu.SemaphoreType.DMA
+    flip = lambda v: jnp.transpose(v, (0, 2, 1, 3))
     nx, pn = pl.pallas_call(
         kernel,
         out_shape=(out, out),
-        in_specs=[vm, vm, vm, vm, pl.BlockSpec(memory_space=pltpu.SMEM)],
+        in_specs=[anywhere] * 10,
         out_specs=(vm, vm),
         scratch_shapes=[
+            V(1, 3, 16, 128), V(1, 3, 16, 128), V(1, 3, 16, 128), pltpu.VMEM((16, 128), jnp.int32), V(216, 32),
+            S((16,), jnp.int32), S((4,), F32), S((4,), F32), S((4,), F32), S((PC, NB), F32),
+            V(5, 16, 128), V(16, 6, 128), V(16, 3, 128), V(16, 128), V(16, 128), V(16, 128), V(16, 128), V(64, 3, 128),
             V(2, 5, 16, 128), V(4, 16, 128, 128), V(3, 16, 128, 128), V(32, 6, 128), V(32, 3, 128),
             V(16, 3, 128), V(3, 72, 128), V(8, 3, 128), V(32, 6, 128), V(16, 6, 128), V(3, 3, 3, 3, 128),
             V(4, 2, 2, 128, 128), V(3, 2, 2, 128, 128), V(4, 3, 128), V(4, 4, 3, 128), V(8, 4, 3, 128), V(8, 4, 3, 128),
-            D((2,)), D((2,)), D((16,)), D, D((16,)), D, D((96,)), D((3,)), D((32,)), D, D((3,)), D, D((8,)), D,
+            D((10,)), D((2,)), D((2,)), D, D, D, D, D, D, D((3,)), D, D, D((3,)), D, D((8,)), D,
         ],
-        compiler_params=pltpu.CompilerParams(collective_id=0, has_side_effects=True, vmem_limit_bytes=40 << 20),
-    )(own, early, aux, jnp.asarray(table), jnp.asarray(weights))
-    return nx[None], pn[None]
+        compiler_params=pltpu.CompilerParams(collective_id=0, has_side_effects=True, vmem_limit_bytes=67043328),
+    )(flip(positions), flip(momenta), flip(noise), atom_types, occupancy, type_sigma, type_eps, type_mass,
+      jnp.asarray(table), jnp.asarray(weights))
+    return flip(nx), flip(pn)
 
 
 def solution(mesh):

time: 78.8 us -> 68.7 us (0.87)
  the two profiles are of different devices: /device:TPU:64 before, /device:TPU:6 now
where the time goes in v2:
time: 68.7 us; the launch traced here: 68.4 us
  Pallas kernels  65.8 us (96%)
  local copies, waits for them, and re-layouts  1.96 us (3%)
    pallas_call x1, Pallas kernels, shards(): pl.pallas_call(kernel, out_shape=(out, out), in_specs=[anywhere] * 10, ou...  65.8 us
    unnamed x4, local copies, waits for them, and re-layouts  1.96 us

profile of v2, /device:TPU:6, one launch (start us, length us, event | category | flops | bytes accessed | tf_op | source)
XLA Modules:
  0.0 68.4 jit_solution(13708167891089056745)
XLA Ops:
  0.6 65.8 %shard_map.113 = (f32[1,3,16,128]{3,2,1,0:T(8,128)}, f32[1,3,16,128]{3,2,1,0:T(8,128)}) custom-call(f32[1,3,16,128]{3,2,1,0:T(8,128)} %bitcast.5, f32[1,3,16,128]{3,2,1,0:T(8,128)} %bitcast.6, f32[1,3,16,128]{3,2,1,0:T(8,128)} %bitcast.7, s32[16,128]{1,0:T(8,128)} %types_in.1, s32[16]{0:T(128)} %occ_in.1, f32[4]{0:T(128)} %sig_in.1, f32[4]{0:T(128)} %eps_in.1, ...), custom_call_target="tpu_custom_call" | custom-call | tf_op jit(solution)/shard_map/pallas_call | solution.py:518
  66.5 0.0 copy-start
  66.5 1.4 %copy.14 = f32[1,16,3,128]{3,1,2,0:T(8,128)} copy(f32[1,16,3,128]{3,1,2,0:T(8,128)} %bitcast.9) | data formatting | bytes 49152
  67.8 0.0 copy-done
  67.8 0.6 copy.15
Async XLA Ops:
  66.5 1.4 %copy-start = (f32[1,3,16,128]{3,2,1,0:T(8,128)S(1)}, f32[1,3,16,128]{3,2,1,0:T(8,128)}, u32[]{:S(2)}) copy-start(f32[1,3,16,128]{3,2,1,0:T(8,128)} %get-tuple-element.5) | copy-start | bytes 73732

commit v3 on v2

--- a/solution.py
+++ b/solution.py
@@ -61,10 +61,10 @@
 
 def kernel(pos_in, mom_in, noise_in, types_in, occ_in, sig_in, eps_in, mass_in, table_in, w_in, nx_ref, np_ref,
            pos, mom, noise, types, table_ref, occ, ts_sig, ts_eps, ts_mass, w_ref,
-           own_ref, early_ref, pm, invm, kcoef, e48, mass, slots,
+           own_ref, early_ref, pm, kcoef, e48, mass, slots, acc_own, acc_j, acc_n, base, react_out, react_in,
            ext, xi, acc, eb, kb, late_out, mixed, cont, ret, rb, cb, xs, sacc, fb, xb, zs, zb,
            in_s, halo_ss, halo_rs, early_ss, early_rs, late_ss, late_rs, cont_ss, cont_own_ss, cont_rs, ret_ss, ret_rs,
-           xb_ss, xb_rs, zb_ss, zb_rs):
+           xb_ss, xb_rs, zb_ss, zb_rs, react_ss, react_rs):
     b = lax.axis_index("bead")
     s = lax.axis_index("space")
     bx = b // 8
@@ -110,9 +110,11 @@
     live = jnp.concatenate([jnp.where(slot_index < occ[c], 1.0, 0.0) for c in range(16)], 0)
     e_all = jnp.sqrt(pick(ts_eps)) * live
     mass[...] = m_all
-    invm[...] = inv
     e48[...] = 48.0 * e_all
-    kcoef[...] = (0.5 * TIME_STEP * 48.0) * e_all * inv
+    kcoef[...] = (0.5 * TIME_STEP * 48.0) * inv
+    for d in range(3):
+        acc_j[d] = jnp.zeros((16, 8, 128), F32)
+        acc_n[d] = jnp.zeros((16, 8, 128), F32)
     root = jnp.sqrt(inv)
     cell_of = lax.broadcasted_iota(jnp.int32, (16, 128), 0)
     corner = (-0.5, (cell_of // 4).astype(F32) - 2.0, (cell_of % 4).astype(F32) - 2.0)
@@ -128,59 +130,86 @@
         return jnp.broadcast_to(ref_row, (128, 128)).T
 
     def prep(c, _):
-        for d in range(4):
+        for d in range(5):
             xi[d, c] = spread(own_ref[d, pl.ds(c, 1), :])
-        for d in range(3):
-            acc[d, c] = jnp.zeros((128, 128), F32)
         return 0
 
     lax.fori_loop(0, 16, prep, 0)
 
-    def short_pairs(src, base_row, y, y2, shift):
+    def right_data(src, row, shift):
+        xj = src(0, row)
+        if shift is not None:
+            xj = xj + shift
+        return [jnp.broadcast_to(v, (8, 128)) for v in (xj, src(1, row), src(2, row), src(3, row), src(4, row))]
+
+    def short_weight(left, right):
+        dx = left[0] - right[0]
+        dy = left[1] - right[1]
+        dz = left[2] - right[2]
+        r2 = dx * dx + dy * dy + dz * dz
+        sp = left[3] + right[3]
+        s2 = sp * sp
+        p = 1.0 / (r2 + s2)
+        m = jnp.maximum(1.0 - r2, 0.0)
+        q = s2 * p
+        w = q * q * q
+        pm_ = p * m
+        bb = pm_ + (2.0 / 3.0)
+        return (w * m) * (w * (pm_ + bb) - bb), dx, dy, dz
+
+    def short_pairs(src, y, y2, shift, init):
         for z in range(4):
             i = y * 4 + z
-            cols = []
-            for z2 in range(max(z - 1, 0), min(z + 2, 4)):
-                row = y2 * 4 + z2
-                xj = src(0, row)
-                if shift is not None:
-                    xj = xj + shift
-                cols.append([jnp.broadcast_to(v, (8, 128)) for v in (xj, src(1, row), src(2, row), src(3, row), src(4, row))])
+            cols = [right_data(src, y2 * 4 + z2, shift) for z2 in range(max(z - 1, 0), min(z + 2, 4))]
             for t in range(16):
                 lanes = pl.ds(8 * t, 8)
-                xa, ya, za, sa = (xi[d, i, lanes, :] for d in range(4))
-                tot = [acc[d, i, lanes, :] for d in range(3)]
-                for xj, yj, zj, sj, ej in cols:
-                    dx = xa - xj
-                    dy = ya - yj
-                    dz = za - zj
-                    r2 = dx * dx + dy * dy + dz * dz
-                    sp = sa + sj
-                    s2 = sp * sp
-                    p = 1.0 / (r2 + s2)
-                    m = jnp.maximum(1.0 - r2, 0.0)
-                    q = s2 * p
-                    w = q * q * q
-                    pm = p * m
-                    bb = pm + (2.0 / 3.0)
-                    g = (w * m) * (w * (pm + bb) - bb) * ej
-                    tot = [tot[0] + g * dx, tot[1] + g * dy, tot[2] + g * dz]
+                left = [xi[d, i, lanes, :] for d in range(4)]
+                tot = None if init else [acc[d, i, lanes, :] for d in range(3)]
+                for right in cols:
+                    g, dx, dy, dz = short_weight(left, right)
+                    g = g * right[4]
+                    add = [g * dx, g * dy, g * dz]
+                    tot = add if tot is None else [u + v for u, v in zip(tot, add)]
                 for d in range(3):
                     acc[d, i, lanes, :] = tot[d]
 
+    def both_ways(src, y, y2, shift, z_lists, same, init, other):
+        for z in range(4):
+            i = y * 4 + z
+            cols = [(z2, right_data(src, y2 * 4 + z2, shift)) for z2 in z_lists[z]]
+            back = {z2: None for z2 in z_lists[z]}
+            for t in range(16):
+                lanes = pl.ds(8 * t, 8)
+                left = [xi[d, i, lanes, :] for d in range(5)]
+                tot = None if init else [acc_own[d, i, lanes, :] for d in range(3)]
+                for z2, right in cols:
+                    g, dx, dy, dz = short_weight(left, right)
+                    g = g * (left[4] * right[4])
+                    add = [g * dx, g * dy, g * dz]
+                    tot = add if tot is None else [u + v for u, v in zip(tot, add)]
+                    if not (same and z2 == z):
+                        back[z2] = add if back[z2] is None else [u + v for u, v in zip(back[z2], add)]
+                for d in range(3):
+                    acc_own[d, i, lanes, :] = tot[d]
+            for z2, got in back.items():
+                if got is not None:
+                    for d in range(3):
+                        other[d, y2 * 4 + z2] = other[d, y2 * 4 + z2] + got[d]
+
+    ALL_Z = [list(range(max(z - 1, 0), min(z + 2, 4))) for z in range(4)]
+    UP_Z = [[z] + ([z + 1] if z < 3 else []) for z in range(4)]
+
     def own_src(d, row):
         return own_ref[d, pl.ds(row, 1), :]
 
-    def own_row(n, _):
-        y = n // 3
-        y2 = y + n % 3 - 1
-
-        @pl.when((y2 >= 0) & (y2 < 4))
-        def _():
-            short_pairs(own_src, None, y, y2, None)
-        return 0
-
-    lax.fori_loop(0, 7, own_row, 0)
+    def same_row(y, _):
+        both_ways(own_src, y, y, None, UP_Z, True, True, acc_j)
+        return 0
+
+
+    def next_row(y, _):
+        both_ways(own_src, y, y + 1, None, ALL_Z, False, False, acc_j)
+        return 0
 
     pl.semaphore_wait(barrier, NB + 1)
 
@@ -220,7 +249,8 @@
         return 0
 
     lax.fori_loop(0, 16, send_early, 0)
-    lax.fori_loop(7, 12, own_row, 0)
+    lax.fori_loop(0, 4, same_row, 0)
+    lax.fori_loop(0, 3, next_row, 0)
 
     def ext_src(k):
         return lambda d, row: ext[k, d, pl.ds(row, 1), :]
@@ -240,19 +270,57 @@
 
     wait_halo(near_side)
 
+    far_space = jnp.where(even, down, up)
+    near_space = jnp.where(even, up, down)
+    near_from = jnp.where(even, 0, 2)
+
     def near_row(n, _):
-        y = n // 3
-        y2 = y + n % 3 - 1
-
-        @pl.when((y2 >= 0) & (y2 < 4))
-        def _():
-            short_pairs(ext_src(near_side), None, y, y2, near_shift)
-        return 0
-
-    lax.fori_loop(0, 12, near_row, 0)
+        y = jnp.where(n < 2, n + near_from, n - 2)
+        y2 = jnp.where(n < 2, y, y + 1)
+        both_ways(ext_src(near_side), y, y2, near_shift, ALL_Z, False, False, acc_n)
+        return 0
+
+    lax.fori_loop(0, 5, near_row, 0)
+    for d in range(3):
+        react_out[d] = -jnp.sum(acc_n[d], 1)
+    react = pltpu.make_async_remote_copy(
+        src_ref=react_out, dst_ref=react_in, send_sem=react_ss, recv_sem=react_rs,
+        device_id={"bead": b, "space": near_space}, device_id_type=MESH)
+    react.start()
+    halo_up.wait_send()
+    halo_down.wait_send()
+    sent_share(early_ref, early_ss)
+    react.wait()
+    for d in range(3):
+        base[d] = react_in[d] - jnp.sum(acc_j[d], 1)
 
     def mm(a, v):
         return jnp.dot(a, v, preferred_element_type=F32, precision=lax.Precision.HIGHEST)
+
+    wait_halo(far_side)
+
+    def far_y(y, _):
+        short_pairs(ext_src(far_side), y, y, far_shift, True)
+
+        def far_row(n, _):
+            y2 = y - 1 + 2 * n
+
+            @pl.when((y2 >= 0) & (y2 < 4))
+            def _():
+                short_pairs(ext_src(far_side), y, y2, far_shift, False)
+            return 0
+
+        lax.fori_loop(0, 2, far_row, 0)
+        for z in range(4):
+            c = y * 4 + z
+            rows = [jnp.sum((acc[d, c] * xi[4, c] + acc_own[d, c]).T, 0, keepdims=True) + base[d, pl.ds(c, 1), :]
+                    for d in range(3)]
+            late_out[c] = pm[c] + kcoef[pl.ds(c, 1), :] * jnp.concatenate(rows, 0)
+        for z in range(4):
+            to_share(late_out, kb, late_ss, late_rs, y * 4 + z)
+        return 0
+
+    lax.fori_loop(0, 4, far_y, 0)
 
     @pl.when(is_share)
     def _():
@@ -260,38 +328,12 @@
         for d in range(3):
             mixed[d] = mm(table_ref[0:72, :], eb[:, d, :]) + mm(table_ref[72:144, :], eb[:, 3 + d, :])
 
-    halo_up.wait_send()
-    halo_down.wait_send()
-    sent_share(early_ref, early_ss)
-    wait_halo(far_side)
-
-    def far_y(y, _):
-        def far_row(n, _):
-            y2 = y + n - 1
-
-            @pl.when((y2 >= 0) & (y2 < 4))
-            def _():
-                short_pairs(ext_src(far_side), None, y, y2, far_shift)
-            return 0
-
-        lax.fori_loop(0, 3, far_row, 0)
-        for z in range(4):
-            c = y * 4 + z
-            rows = [jnp.sum(acc[d, c].T, 0, keepdims=True) for d in range(3)]
-            late_out[c] = pm[c] + kcoef[pl.ds(c, 1), :] * jnp.concatenate(rows, 0)
-        for z in range(4):
-            to_share(late_out, kb, late_ss, late_rs, y * 4 + z)
-        return 0
-
-    lax.fori_loop(0, 4, far_y, 0)
 
     my_y = my_cell // 4
     my_z = my_cell % 4
     y_first, y_last = jnp.where(my_y == 3, 1, 0), jnp.where(my_y == 0, 1, 2)
     z_first, z_last = jnp.where(my_z == 3, 1, 0), jnp.where(my_z == 0, 1, 2)
     blocks = (y_last - y_first) * (z_last - z_first)
-    far_space = jnp.where(even, down, up)
-    near_space = jnp.where(even, up, down)
     far_dst = jnp.where(even, 2, 0)
     near_dst = jnp.where(even, 0, 2)
     my_r = (bz8 // 4) * 4 + bx
@@ -322,9 +364,6 @@
                         device_id={"bead": (r % 4) * 8 + (r // 4) * 4 + q, "space": space}, device_id_type=MESH).start()
             over_blocks(body)
 
-        outside(far_space, far_dst)
-        outside(near_space, near_dst)
-
         def inside(q, jy, jz):
             for r in range(PC):
                 tb = (r % 4) * 8 + (r // 4) * 4 + q
@@ -340,6 +379,8 @@
                     pltpu.make_async_copy(cont.at[r], cb.at[1, jy, jz], cont_rs.at[1]).start()
 
         over_blocks(inside)
+        outside(near_space, near_dst)
+        outside(far_space, far_dst)
         for d in range(3):
             full = mixed[d, 0:64, :] + mm(table_ref[144:208, :], kb[:, d, :])
             ret[:, d, :] = full[0:32]
@@ -523,11 +564,12 @@
         scratch_shapes=[
             V(1, 3, 16, 128), V(1, 3, 16, 128), V(1, 3, 16, 128), pltpu.VMEM((16, 128), jnp.int32), V(216, 32),
             S((16,), jnp.int32), S((4,), F32), S((4,), F32), S((4,), F32), S((PC, NB), F32),
-            V(5, 16, 128), V(16, 6, 128), V(16, 3, 128), V(16, 128), V(16, 128), V(16, 128), V(16, 128), V(64, 3, 128),
-            V(2, 5, 16, 128), V(4, 16, 128, 128), V(3, 16, 128, 128), V(32, 6, 128), V(32, 3, 128),
+            V(5, 16, 128), V(16, 6, 128), V(16, 3, 128), V(16, 128), V(16, 128), V(16, 128), V(64, 3, 128),
+            V(3, 16, 128, 128), V(3, 16, 8, 128), V(3, 16, 8, 128), V(3, 16, 128), V(3, 16, 128), V(3, 16, 128),
+            V(2, 5, 16, 128), V(5, 16, 128, 128), V(3, 16, 128, 128), V(32, 6, 128), V(32, 3, 128),
             V(16, 3, 128), V(3, 72, 128), V(8, 3, 128), V(32, 6, 128), V(16, 6, 128), V(3, 3, 3, 3, 128),
             V(4, 2, 2, 128, 128), V(3, 2, 2, 128, 128), V(4, 3, 128), V(4, 4, 3, 128), V(8, 4, 3, 128), V(8, 4, 3, 128),
-            D((10,)), D((2,)), D((2,)), D, D, D, D, D, D, D((3,)), D, D, D((3,)), D, D((8,)), D,
+            D((10,)), D((2,)), D((2,)), D, D, D, D, D, D, D((3,)), D, D, D((3,)), D, D((8,)), D, D, D,
         ],
         compiler_params=pltpu.CompilerParams(collective_id=0, has_side_effects=True, vmem_limit_bytes=67043328),
     )(flip(positions), flip(momenta), flip(noise), atom_types, occupancy, type_sigma, type_eps, type_mass,

time: 68.7 us -> 66.6 us (0.969)
  Pallas kernels: 65.8 us -> 63.8 us
    pallas_call x1, Pallas kernels: 65.8 us -> 63.8 us  [shards(): pl.pallas_call(kernel, out_shape=(out, out), in_specs=[anywhere] * 10, ou...]
where the time goes in v3:
time: 66.6 us; the launch traced here: 66.4 us
  Pallas kernels  63.8 us (96%)
  local copies, waits for them, and re-layouts  1.96 us (3%)
    pallas_call x1, Pallas kernels, shards(): pl.pallas_call(kernel, out_shape=(out, out), in_specs=[anywhere] * 10, ou...  63.8 us
    unnamed x4, local copies, waits for them, and re-layouts  1.96 us

profile of v3, /device:TPU:6, one launch (start us, length us, event | category | flops | bytes accessed | tf_op | source)
XLA Modules:
  0.0 66.4 jit_solution(8513932237560298100)
XLA Ops:
  0.6 63.8 %shard_map.113 = (f32[1,3,16,128]{3,2,1,0:T(8,128)}, f32[1,3,16,128]{3,2,1,0:T(8,128)}) custom-call(f32[1,3,16,128]{3,2,1,0:T(8,128)} %bitcast.5, f32[1,3,16,128]{3,2,1,0:T(8,128)} %bitcast.6, f32[1,3,16,128]{3,2,1,0:T(8,128)} %bitcast.7, s32[16,128]{1,0:T(8,128)} %types_in.1, s32[16]{0:T(128)} %occ_in.1, f32[4]{0:T(128)} %sig_in.1, f32[4]{0:T(128)} %eps_in.1, ...), custom_call_target="tpu_custom_call" | custom-call | tf_op jit(solution)/shard_map/pallas_call | solution.py:559
  64.4 0.0 copy-start
  64.5 1.4 %copy.14 = f32[1,16,3,128]{3,1,2,0:T(8,128)} copy(f32[1,16,3,128]{3,1,2,0:T(8,128)} %bitcast.9) | data formatting | bytes 49152
  65.8 0.0 copy-done
  65.8 0.6 copy.15
Async XLA Ops:
  64.4 1.4 %copy-start = (f32[1,3,16,128]{3,2,1,0:T(8,128)S(1)}, f32[1,3,16,128]{3,2,1,0:T(8,128)}, u32[]{:S(2)}) copy-start(f32[1,3,16,128]{3,2,1,0:T(8,128)} %get-tuple-element.5) | copy-start | bytes 73732

commit v4 on v3

--- a/solution.py
+++ b/solution.py
@@ -59,15 +59,16 @@
     return (cell // 4) * 8 + 2 + cell % 4
 
 
-def kernel(pos_in, mom_in, noise_in, types_in, occ_in, sig_in, eps_in, mass_in, table_in, w_in, nx_ref, np_ref,
+def kernel(pos_in, mom_in, noise_in, types_in, occ_in, sig_in, eps_in, mass_in, table_in, w_in, both_ref,
            pos, mom, noise, types, table_ref, occ, ts_sig, ts_eps, ts_mass, w_ref,
-           own_ref, early_ref, pm, kcoef, e48, mass, slots, acc_own, acc_j, acc_n, base, react_out, react_in,
-           ext, xi, acc, eb, kb, late_out, mixed, cont, ret, rb, cb, xs, sacc, fb, xb, zs, zb,
+           own_ref, early_ref, pm, kcoef, mass, slots, acc_own, acc_j, acc_n, base, react_out, react_in,
+           ext, xi, acc, eb, kb, late_out, mixed, cont, ret, rb, cb, xs, sacc, sacc2, sback, fb, xb, zs, zb,
            in_s, halo_ss, halo_rs, early_ss, early_rs, late_ss, late_rs, cont_ss, cont_own_ss, cont_rs, ret_ss, ret_rs,
            xb_ss, xb_rs, zb_ss, zb_rs, react_ss, react_rs):
     b = lax.axis_index("bead")
     s = lax.axis_index("space")
     bx = b // 8
+    nx_ref, np_ref = both_ref.at[0], both_ref.at[1]
     bz8 = b % 8
     up = (s + 1) % NS
     down = (s + NS - 1) % NS
@@ -110,7 +111,6 @@
     live = jnp.concatenate([jnp.where(slot_index < occ[c], 1.0, 0.0) for c in range(16)], 0)
     e_all = jnp.sqrt(pick(ts_eps)) * live
     mass[...] = m_all
-    e48[...] = 48.0 * e_all
     kcoef[...] = (0.5 * TIME_STEP * 48.0) * inv
     for d in range(3):
         acc_j[d] = jnp.zeros((16, 8, 128), F32)
@@ -409,64 +409,104 @@
     def wait_cont(slot):
         pltpu.make_async_copy(cb.at[slot], cb.at[slot], cont_rs.at[slot]).wait()
 
+    def block_cell(n):
+        return flip(by, n // 2, 1), flip(bz, n % 2, 1)
+
     wait_cont(1)
-    for iy in range(2):
-        for iz in range(2):
-            wy = by + iy
-            wz = bz + iz
-            me = cb[1, wy, wz]
-            cell = (2 * by + iy) * 4 + 2 * bz + iz
-            xs[0, iy, iz] = spread(2.0 * me[0:1])
-            xs[1, iy, iz] = spread(2.0 * (me[1:2] + wy.astype(F32)))
-            xs[2, iy, iz] = spread(2.0 * (me[2:3] + wz.astype(F32)))
-            xs[3, iy, iz] = spread(own_ref[3, pl.ds(cell, 1), :])
+    for n in range(4):
+        iy, iz = block_cell(n)
+        wy = by + iy
+        wz = bz + iz
+        me = cb[1, wy, wz]
+        cell = (2 * by + iy) * 4 + 2 * bz + iz
+        xs[0, n] = spread(2.0 * me[0:1])
+        xs[1, n] = spread(2.0 * (me[1:2] + wy.astype(F32)))
+        xs[2, n] = spread(2.0 * (me[2:3] + wz.astype(F32)))
+        xs[3, n] = spread(own_ref[3, pl.ds(cell, 1), :])
+        xs[4, n] = spread(own_ref[4, pl.ds(cell, 1), :])
+
+    def window_data(slot, params, shift, jy0, jz0):
+        jy = flip(by, jy0, 2)
+        jz = flip(bz, jz0, 2)
+        v = cb[slot, jy, jz]
+        row = (by + jy) * 4 + bz + jz
+        vals = (2.0 * v[0:1] + shift, 2.0 * (v[1:2] + jnp.asarray(jy).astype(F32)), 2.0 * (v[2:3] + jnp.asarray(jz).astype(F32)), params(3, row), params(4, row))
+        return [jnp.broadcast_to(a, (8, 128)) for a in vals]
+
+    def long_weight(left, right):
+        dx = left[0] - right[0]
+        dy = left[1] - right[1]
+        dz = left[2] - right[2]
+        r2 = dx * dx + dy * dy + dz * dz
+        sp = left[3] + right[3]
+        s2 = sp * sp
+        p = 1.0 / (r2 + s2)
+        outer = jnp.maximum(4.0 - r2, 0.0)
+        inner = jnp.maximum(1.0 - r2, 0.0)
+        inner16 = 16.0 * inner
+        w = s2 * p
+        w = w * w * w
+        ps = p * (outer * outer - inner16 * inner)
+        bb = ps + (outer - inner16) * (2.0 / 3.0)
+        return w * (w * (ps + bb) - bb), dx, dy, dz
+
+    def plus(tot, add):
+        return add if tot is None else [u + v for u, v in zip(tot, add)]
+
+    window = {(jy, jz): window_data(1, own_src, 0.0, jy, jz) for jy in range(3) for jz in range(3)}
+    for n in range(4):
+        sides = [(jy, jz) for jy in range(3) for jz in range(3)
+                 if abs(jy - n // 2) <= 1 and abs(jz - n % 2) <= 1]
+        single = [j for j in sides if 2 in j or j == (n // 2, n % 2)]
+        double = [j for j in sides if 2 not in j and j[0] * 2 + j[1] > n]
+        back = {j: None for j in double}
+        for t in range(16):
+            lanes = pl.ds(8 * t, 8)
+            left = [xs[d, n, lanes, :] for d in range(5)]
+            tot = tot2 = None
+            for j in single:
+                g, dx, dy, dz = long_weight(left, window[j])
+                g = g * window[j][4]
+                tot = plus(tot, [g * dx, g * dy, g * dz])
+            for j in double:
+                g, dx, dy, dz = long_weight(left, window[j])
+                g = g * (left[4] * window[j][4])
+                add = [g * dx, g * dy, g * dz]
+                tot2 = plus(tot2, add)
+                back[j] = plus(back[j], add)
             for d in range(3):
-                sacc[d, iy, iz] = jnp.zeros((128, 128), F32)
-
-    Y_PAIRS = ((0, 0), (0, 1), (1, 0), (1, 1), (1, 2))
+                sacc[d, n, lanes, :] = tot[d]
+                if double:
+                    sacc2[d, n, lanes, :] = tot2[d]
+        for k, j in enumerate(double):
+            at = j[0] * 2 + j[1]
+            for d in range(3):
+                if n == 0:
+                    sback[d, at] = back[j][d]
+                else:
+                    sback[d, at] = sback[d, at] + back[j][d]
 
     def slow_pairs(slot, params, shift):
         def one(n, _):
             fy = jnp.where(n < 2, 0, 1)
-            jy = flip(by, jnp.where(n < 2, n, n - 2), 2)
-            iy = flip(by, fy, 1)
-            js = []
-            for jz0 in range(3):
-                jz = flip(bz, jz0, 2)
-                v = cb[slot, jy, jz]
-                row = (by + jy) * 4 + bz + jz
-                vals = (2.0 * v[0:1] + shift, 2.0 * (v[1:2] + jy.astype(F32)), 2.0 * (v[2:3] + jz.astype(F32)), params(3, row), params(4, row))
-                js.append([jnp.broadcast_to(a, (8, 128)) for a in vals])
+            jy0 = jnp.where(n < 2, n, n - 2)
+            js = [window_data(slot, params, shift, jy0, jz0) for jz0 in range(3)]
             for iz0 in range(2):
-                iz = flip(bz, iz0, 1)
+                at = fy * 2 + iz0
                 for t in range(16):
                     lanes = pl.ds(8 * t, 8)
-                    xa, ya, za, sa = (xs[d, iy, iz, lanes, :] for d in range(4))
-                    tot = [sacc[d, iy, iz, lanes, :] for d in range(3)]
+                    left = [xs[d, at, lanes, :] for d in range(4)]
+                    tot = [sacc[d, at, lanes, :] for d in range(3)]
                     for jz0 in (range(2) if iz0 == 0 else range(3)):
-                        xj, yj, zj, sj, ej = js[jz0]
-                        dx = xa - xj
-                        dy = ya - yj
-                        dz = za - zj
-                        r2 = dx * dx + dy * dy + dz * dz
-                        sp = sa + sj
-                        s2 = sp * sp
-                        p = 1.0 / (r2 + s2)
-                        m2 = jnp.maximum(1.0 - r2, 0.0)
-                        m1 = jnp.maximum(1.0 - 0.25 * r2, 0.0)
-                        w = s2 * p
-                        w = w * w * w
-                        ps = p * (m1 * m1 - m2 * m2)
-                        bb = ps + (m1 * (1.0 / 6.0) - m2 * (2.0 / 3.0))
-                        g = w * (w * (ps + bb) - bb) * ej
+                        g, dx, dy, dz = long_weight(left, js[jz0])
+                        g = g * js[jz0][4]
                         tot = [tot[0] + g * dx, tot[1] + g * dy, tot[2] + g * dz]
                     for d in range(3):
-                        sacc[d, iy, iz, lanes, :] = tot[d]
+                        sacc[d, at, lanes, :] = tot[d]
             return 0
 
         lax.fori_loop(0, 5, one, 0)
 
-    slow_pairs(1, own_src, 0.0)
     near_slot = near_side * 2
     far_slot = far_side * 2
     wait_cont(near_slot)
@@ -474,11 +514,18 @@
     wait_cont(far_slot)
     slow_pairs(far_slot, ext_src(far_side), far_shift)
 
-    for iy in range(2):
-        for iz in range(2):
-            cell = (2 * by + iy) * 4 + 2 * bz + iz
-            rows = [jnp.sum(sacc[d, iy, iz].T, 0, keepdims=True) for d in range(3)]
-            fb[2 * iy + iz] = e48[pl.ds(cell, 1), :] * jnp.concatenate(rows, 0)
+    for n in range(4):
+        iy, iz = block_cell(n)
+        rows = []
+        for d in range(3):
+            lanes = sacc[d, n] * xs[4, n]
+            if n < 3:
+                lanes = lanes + sacc2[d, n]
+            row = jnp.sum(lanes.T, 0, keepdims=True)
+            if n > 0:
+                row = row - jnp.sum(sback[d, n], 0, keepdims=True)
+            rows.append(3.0 * row)
+        fb[2 * iy + iz] = jnp.concatenate(rows, 0)
 
     def x_copy(i):
         other = (bx + 1 + i) % 4
@@ -556,25 +603,25 @@
     S = lambda shape, kind: pltpu.SMEM(shape, kind)
     D = pltpu.SemaphoreType.DMA
     flip = lambda v: jnp.transpose(v, (0, 2, 1, 3))
-    nx, pn = pl.pallas_call(
+    both = pl.pallas_call(
         kernel,
-        out_shape=(out, out),
+        out_shape=jax.ShapeDtypeStruct((2, 1, 3, 16, 128), F32),
         in_specs=[anywhere] * 10,
-        out_specs=(vm, vm),
+        out_specs=vm,
         scratch_shapes=[
             V(1, 3, 16, 128), V(1, 3, 16, 128), V(1, 3, 16, 128), pltpu.VMEM((16, 128), jnp.int32), V(216, 32),
             S((16,), jnp.int32), S((4,), F32), S((4,), F32), S((4,), F32), S((PC, NB), F32),
-            V(5, 16, 128), V(16, 6, 128), V(16, 3, 128), V(16, 128), V(16, 128), V(16, 128), V(64, 3, 128),
+            V(5, 16, 128), V(16, 6, 128), V(16, 3, 128), V(16, 128), V(16, 128), V(64, 3, 128),
             V(3, 16, 128, 128), V(3, 16, 8, 128), V(3, 16, 8, 128), V(3, 16, 128), V(3, 16, 128), V(3, 16, 128),
             V(2, 5, 16, 128), V(5, 16, 128, 128), V(3, 16, 128, 128), V(32, 6, 128), V(32, 3, 128),
             V(16, 3, 128), V(3, 72, 128), V(8, 3, 128), V(32, 6, 128), V(16, 6, 128), V(3, 3, 3, 3, 128),
-            V(4, 2, 2, 128, 128), V(3, 2, 2, 128, 128), V(4, 3, 128), V(4, 4, 3, 128), V(8, 4, 3, 128), V(8, 4, 3, 128),
+            V(5, 4, 128, 128), V(3, 4, 128, 128), V(3, 3, 128, 128), V(3, 4, 8, 128), V(4, 3, 128), V(4, 4, 3, 128), V(8, 4, 3, 128), V(8, 4, 3, 128),
             D((10,)), D((2,)), D((2,)), D, D, D, D, D, D, D((3,)), D, D, D((3,)), D, D((8,)), D, D, D,
         ],
         compiler_params=pltpu.CompilerParams(collective_id=0, has_side_effects=True, vmem_limit_bytes=67043328),
     )(flip(positions), flip(momenta), flip(noise), atom_types, occupancy, type_sigma, type_eps, type_mass,
       jnp.asarray(table), jnp.asarray(weights))
-    return flip(nx), flip(pn)
+    return flip(both[0]), flip(both[1])
 
 
 def solution(mesh):

time: 66.6 us -> 65.1 us (0.977)
  Pallas kernels: 63.8 us -> 62.9 us
    unnamed x4 -> x0, local copies, waits for them, and re-layouts: 1.96 us -> none
    transpose x0 -> x1, local copies, waits for them, and re-layouts: none -> 1.38 us  [shards(): flip = lambda v: jnp.transpose(v, (0, 2, 1, 3))]
    pallas_call x1, Pallas kernels: 63.8 us -> 62.9 us  [shards(): pl.pallas_call(kernel, out_shape=jax.ShapeDtypeStruct((2, 1, 3, 16, 128),...]
where the time goes in v4:
time: 65.1 us; the launch traced here: 64.9 us
  Pallas kernels  62.9 us (97%)
  local copies, waits for them, and re-layouts  1.38 us (2%)
    pallas_call x1, Pallas kernels, shards(): pl.pallas_call(kernel, out_shape=jax.ShapeDtypeStruct((2, 1, 3, 16, 128),...  62.9 us
    transpose x1, local copies, waits for them, and re-layouts, shards(): flip = lambda v: jnp.transpose(v, (0, 2, 1, 3))  1.38 us

profile of v4, /device:TPU:6, one launch (start us, length us, event | category | flops | bytes accessed | tf_op | source)
XLA Modules:
  0.0 64.9 jit_solution(5775999288473493387)
XLA Ops:
  0.6 62.9 %shard_map.113 = f32[2,1,3,16,128]{4,3,2,1,0:T(8,128)} custom-call(f32[1,3,16,128]{3,2,1,0:T(8,128)} %bitcast.11, f32[1,3,16,128]{3,2,1,0:T(8,128)} %bitcast.12, f32[1,3,16,128]{3,2,1,0:T(8,128)} %bitcast.13, s32[16,128]{1,0:T(8,128)} %types_in.1, s32[16]{0:T(128)} %occ_in.1, f32[4]{0:T(128)} %sig_in.1, f32[4]{0:T(128)} %eps_in.1, f32[4]{0:T(128)} %mass_in.1, ...), custom_call_target="tpu_custom_call" | custom-call | tf_op jit(solution)/shard_map/pallas_call | solution.py:606
  63.5 1.4 %slice_bitcast_fusion = (f32[1,16,3,128]{3,1,2,0:T(8,128)}, f32[1,16,3,128]{3,1,2,0:T(8,128)}) fusion(f32[2,1,3,16,128]{4,3,2,1,0:T(8,128)} %shard_map.113), kind=kLoop, calls=%fused_computation | loop fusion | bytes 98304 | tf_op jit(solution)/shard_map/transpose | solution.py:605

commit v5 on v4

--- a/solution.py
+++ b/solution.py
@@ -213,14 +213,16 @@
 
     pl.semaphore_wait(barrier, NB + 1)
 
-    halo_up = pltpu.make_async_remote_copy(
-        src_ref=own_ref, dst_ref=ext.at[0], send_sem=halo_ss.at[0], recv_sem=halo_rs.at[0],
-        device_id={"bead": b, "space": up}, device_id_type=MESH)
-    halo_down = pltpu.make_async_remote_copy(
-        src_ref=own_ref, dst_ref=ext.at[1], send_sem=halo_ss.at[1], recv_sem=halo_rs.at[1],
-        device_id={"bead": b, "space": down}, device_id_type=MESH)
-    halo_up.start()
-    halo_down.start()
+    def halo(side, part):
+        cells = pl.ds(8 * part, 8)
+        return pltpu.make_async_remote_copy(
+            src_ref=own_ref.at[:, cells, :], dst_ref=ext.at[side, :, cells, :],
+            send_sem=halo_ss.at[side, part], recv_sem=halo_rs.at[side, part],
+            device_id={"bead": b, "space": jnp.where(side == 0, up, down)}, device_id_type=MESH)
+
+    for part in range(2):
+        for side in range(2):
+            halo(side, part).start()
 
     def to_share(src, dst, ss, rs, c):
         target = share_bead(c)
@@ -254,11 +256,6 @@
 
     def ext_src(k):
         return lambda d, row: ext[k, d, pl.ds(row, 1), :]
-
-    def wait_halo(side):
-        pltpu.make_async_remote_copy(
-            src_ref=own_ref, dst_ref=ext.at[side], send_sem=halo_ss.at[side], recv_sem=halo_rs.at[side],
-            device_id={"bead": b, "space": up}, device_id_type=MESH).wait_recv()
 
     def both(which):
         side = jnp.where(even, 1 - which, which)
@@ -268,7 +265,8 @@
     near_side, near_shift = both(0)
     far_side, far_shift = both(1)
 
-    wait_halo(near_side)
+    halo(near_side, 0).wait_recv()
+    halo(near_side, 1).wait_recv()
 
     far_space = jnp.where(even, down, up)
     near_space = jnp.where(even, up, down)
@@ -287,8 +285,9 @@
         src_ref=react_out, dst_ref=react_in, send_sem=react_ss, recv_sem=react_rs,
         device_id={"bead": b, "space": near_space}, device_id_type=MESH)
     react.start()
-    halo_up.wait_send()
-    halo_down.wait_send()
+    for part in range(2):
+        for side in range(2):
+            halo(side, part).wait_send()
     sent_share(early_ref, early_ss)
     react.wait()
     for d in range(3):
@@ -297,9 +296,13 @@
     def mm(a, v):
         return jnp.dot(a, v, preferred_element_type=F32, precision=lax.Precision.HIGHEST)
 
-    wait_halo(far_side)
+    halo(far_side, 0).wait_recv()
 
     def far_y(y, _):
+        @pl.when(y == 1)
+        def _():
+            halo(far_side, 1).wait_recv()
+
         short_pairs(ext_src(far_side), y, y, far_shift, True)
 
         def far_row(n, _):
@@ -616,7 +619,7 @@
             V(2, 5, 16, 128), V(5, 16, 128, 128), V(3, 16, 128, 128), V(32, 6, 128), V(32, 3, 128),
             V(16, 3, 128), V(3, 72, 128), V(8, 3, 128), V(32, 6, 128), V(16, 6, 128), V(3, 3, 3, 3, 128),
             V(5, 4, 128, 128), V(3, 4, 128, 128), V(3, 3, 128, 128), V(3, 4, 8, 128), V(4, 3, 128), V(4, 4, 3, 128), V(8, 4, 3, 128), V(8, 4, 3, 128),
-            D((10,)), D((2,)), D((2,)), D, D, D, D, D, D, D((3,)), D, D, D((3,)), D, D((8,)), D, D, D,
+            D((10,)), D((2, 2)), D((2, 2)), D, D, D, D, D, D, D((3,)), D, D, D((3,)), D, D((8,)), D, D, D,
         ],
         compiler_params=pltpu.CompilerParams(collective_id=0, has_side_effects=True, vmem_limit_bytes=67043328),
     )(flip(positions), flip(momenta), flip(noise), atom_types, occupancy, type_sigma, type_eps, type_mass,

time: 65.1 us -> 63.9 us (0.982)
  Pallas kernels: 62.9 us -> 61.7 us
    pallas_call x1, Pallas kernels: 62.9 us -> 61.7 us  [shards(): pl.pallas_call(kernel, out_shape=jax.ShapeDtypeStruct((2, 1, 3, 16, 128),...]
where the time goes in v5:
time: 63.9 us; the launch traced here: 63.7 us
  Pallas kernels  61.7 us (97%)
  local copies, waits for them, and re-layouts  1.38 us (2%)
  between operations  0.64 us (1%)
    pallas_call x1, Pallas kernels, shards(): pl.pallas_call(kernel, out_shape=jax.ShapeDtypeStruct((2, 1, 3, 16, 128),...  61.7 us
    transpose x1, local copies, waits for them, and re-layouts, shards(): flip = lambda v: jnp.transpose(v, (0, 2, 1, 3))  1.38 us

profile of v5, /device:TPU:6, one launch (start us, length us, event | category | flops | bytes accessed | tf_op | source)
XLA Modules:
  0.0 63.7 jit_solution(16785344831699772315)
XLA Ops:
  0.6 61.7 %shard_map.113 = f32[2,1,3,16,128]{4,3,2,1,0:T(8,128)} custom-call(f32[1,3,16,128]{3,2,1,0:T(8,128)} %bitcast.11, f32[1,3,16,128]{3,2,1,0:T(8,128)} %bitcast.12, f32[1,3,16,128]{3,2,1,0:T(8,128)} %bitcast.13, s32[16,128]{1,0:T(8,128)} %types_in.1, s32[16]{0:T(128)} %occ_in.1, f32[4]{0:T(128)} %sig_in.1, f32[4]{0:T(128)} %eps_in.1, f32[4]{0:T(128)} %mass_in.1, ...), custom_call_target="tpu_custom_call" | custom-call | tf_op jit(solution)/shard_map/pallas_call | solution.py:609
  62.3 1.4 %slice_bitcast_fusion = (f32[1,16,3,128]{3,1,2,0:T(8,128)}, f32[1,16,3,128]{3,1,2,0:T(8,128)}) fusion(f32[2,1,3,16,128]{4,3,2,1,0:T(8,128)} %shard_map.113), kind=kLoop, calls=%fused_computation | loop fusion | bytes 98304 | tf_op jit(solution)/shard_map/transpose | solution.py:608
